TPU v7x, 32 devices: a whole 2x2x4 slice. The times are simulated.
32 devices in a mesh: seq: 8 (over z, y), dp: 4 (over x, core).
Axes of the slice: x: 2, y: 2, z: 4, core: 2. Of those that a mesh axis runs over, the one named last changes fastest.
Arguments:
- byte_states: bfloat16 [4, 2048, 4096], P('dp', 'seq'), may hold values from -16 to 16
- byte_patch: int32 [4, 2048], P('dp', 'seq'), may hold values from 0 to 575, as said below
- patch_owner: int32 [4, 576], P('dp'), may hold values from 0 to 7, as said below
- qkv_weight: bfloat16 [4096, 3072], P(None, 'dp'), may hold values from -0.09375 to 0.09375
- attention_output_gradient: bfloat16 [4, 576, 2048], P('dp', 'seq'), may hold values from -6 to 6
Outputs:
- attention: bfloat16 [4, 576, 2048], P('dp', 'seq')
- state_grad: bfloat16 [4, 2048, 4096], P('dp', 'seq')
- weight_grad: float32 [4096, 3072], P('seq', 'dp')
Inputs may be any that keep to these rules, and one draw needn't show every extreme that they name: `byte_patch`: patch numbers never fall along a sequence, every patch lies within the bytes of one index of seq, and every patch number is used. One index of seq in each sequence, drawn, holds 128 patches of two bytes; every other index holds 64 patches in consecutive pairs that together hold 8 bytes, each patch 1 to 7 bytes. `patch_owner`: patches 0 to 7, 8 to 15 and so on form groups in which every owner appears exactly once.
All inputs are finite; a program needn't handle non-finite values.
Results may differ from a plain program's by a relative error of at most 0.028.
Values may be sent and summed in bfloat16 or wider, within the bound.
No kernel may reach another device: no remote copies, remote signals or barrier semaphores. Data moves between devices by JAX's collectives and lax.ppermute only.
A program may use at most 128 MiB of HBM per device.

v0:
```python
import jax
import jax.numpy as jnp
from jax import lax
from jax.sharding import PartitionSpec as P

QUERY_HEADS = 16
KEY_VALUE_HEADS = 4
HEAD_SIZE = 128


def contract_rows(left, right):
    return lax.dot_general(
        left, right, (((0,), (0,)), ((), ())), preferred_element_type=jnp.float32
    )


def body(byte_states, byte_patch, patch_owner, qkv_weight, attention_output_gradient):
    seq_count = lax.axis_size("seq")
    byte_rows = byte_states[0]
    byte_total = byte_rows.shape[0]
    slot_count = byte_total // 2
    capacity = slot_count // seq_count
    owner_row_list = attention_output_gradient.shape[1]
    patch_ids = byte_patch[0]
    first_patch = patch_ids[0]
    slot_range = jnp.arange(slot_count, dtype=jnp.int32)
    local_ids = patch_ids - first_patch
    onehot = local_ids[None, :] == slot_range[:, None]
    onehot_low = onehot.astype(jnp.bfloat16)
    summed = jnp.dot(onehot_low, byte_rows, preferred_element_type=jnp.float32)
    counts = jnp.sum(onehot.astype(jnp.float32), axis=1)
    pooled = (summed / jnp.maximum(counts, 1.0)[:, None]).astype(jnp.bfloat16)
    padded_owner = jnp.concatenate([patch_owner[0], jnp.zeros((slot_count,), jnp.int32)])
    owners_here = lax.dynamic_slice_in_dim(padded_owner, first_patch, slot_count)
    valid_slot = counts > 0.0
    target_slot = owners_here * capacity + slot_range // seq_count
    send_range = jnp.arange(seq_count * capacity, dtype=jnp.int32)
    routing = (target_slot[None, :] == send_range[:, None]) & valid_slot[None, :]
    routing_low = routing.astype(jnp.bfloat16)
    send_rows = jnp.dot(routing_low, pooled, preferred_element_type=jnp.float32).astype(
        jnp.bfloat16
    )
    send_index = (
        jnp.sum(jnp.where(routing, (first_patch + slot_range)[None, :], 0), axis=1)
        - 1
        + jnp.any(routing, axis=1).astype(jnp.int32)
    )
    recv_rows, recv_index = (
        lax.all_to_all(
            send_rows.reshape(seq_count, capacity, -1),
            "seq",
            split_axis=0,
            concat_axis=0,
            tiled=True,
        ),
        lax.all_to_all(
            send_index.reshape(seq_count, capacity), "seq", split_axis=0, concat_axis=0, tiled=True
        ),
    )
    flat_rows = recv_rows.reshape(seq_count * capacity, -1)
    flat_index = recv_index.reshape(-1)
    row_range = jnp.arange(owner_row_list, dtype=jnp.int32)
    collect = (flat_index[None, :] // seq_count == row_range[:, None]) & (flat_index[None, :] >= 0)
    collect_low = collect.astype(jnp.bfloat16)
    own_rows = jnp.dot(collect_low, flat_rows, preferred_element_type=jnp.float32).astype(
        jnp.bfloat16
    )
    own_index = jnp.sum(jnp.where(collect, flat_index[None, :], 0), axis=1)
    all_rows = lax.all_gather(own_rows, "dp", axis=0, tiled=True)
    proj_cols = jnp.dot(all_rows, qkv_weight, preferred_element_type=jnp.float32).astype(
        jnp.bfloat16
    )
    projected_states = lax.all_to_all(proj_cols, "dp", split_axis=0, concat_axis=1, tiled=True)
    query_group_size = QUERY_HEADS // KEY_VALUE_HEADS
    query_row_width = QUERY_HEADS * HEAD_SIZE
    key_row_width = KEY_VALUE_HEADS * HEAD_SIZE
    query_rows = projected_states[:, :query_row_width].reshape(
        owner_row_list, KEY_VALUE_HEADS, query_group_size, HEAD_SIZE
    )
    key_value = projected_states[:, query_row_width:]
    all_pair_list, every_index = (
        lax.all_gather(key_value, "seq", axis=0, tiled=True),
        lax.all_gather(own_index, "seq", axis=0, tiled=True),
    )
    total_patches = all_pair_list.shape[0]
    key_head_count = all_pair_list[:, :key_row_width].reshape(
        total_patches, KEY_VALUE_HEADS, HEAD_SIZE
    )
    value_rows = all_pair_list[:, key_row_width:].reshape(total_patches, KEY_VALUE_HEADS, HEAD_SIZE)
    factor = HEAD_SIZE ** (-0.5)
    scores = (
        jnp.einsum("qhgd,khd->hgqk", query_rows, key_head_count, preferred_element_type=jnp.float32)
        * factor
    )
    allowed = every_index[None, :] <= own_index[:, None]
    scores = jnp.where(allowed[None, None], scores, -jnp.inf)
    row_peak = jnp.max(scores, axis=-1, keepdims=True)
    shifted = jnp.exp(scores - row_peak)
    attend = shifted / jnp.sum(shifted, axis=-1, keepdims=True)
    attended_lower = attend.astype(jnp.bfloat16)
    attended = jnp.einsum(
        "hgqk,khd->qhgd", attended_lower, value_rows, preferred_element_type=jnp.float32
    )
    attn_rows = attended.reshape(owner_row_list, query_row_width).astype(jnp.bfloat16)
    gradient_row_list = attention_output_gradient[0].reshape(
        owner_row_list, KEY_VALUE_HEADS, query_group_size, HEAD_SIZE
    )
    grad_attend = jnp.einsum(
        "qhgd,khd->hgqk", gradient_row_list, value_rows, preferred_element_type=jnp.float32
    )
    row_delta = jnp.einsum("qhgd,qhgd->hgq", gradient_row_list.astype(jnp.float32), attended)
    score_gradient = (attend * (grad_attend - row_delta[..., None])).astype(jnp.bfloat16)
    grad_values = jnp.einsum(
        "hgqk,qhgd->khd", attended_lower, gradient_row_list, preferred_element_type=jnp.float32
    )
    grad_keys = (
        jnp.einsum("hgqk,qhgd->khd", score_gradient, query_rows, preferred_element_type=jnp.float32)
        * factor
    )
    grad_queries = (
        jnp.einsum(
            "hgqk,khd->qhgd", score_gradient, key_head_count, preferred_element_type=jnp.float32
        )
        * factor
    )
    key_terms = jnp.concatenate(
        [
            grad_keys.reshape(total_patches, key_row_width),
            grad_values.reshape(total_patches, key_row_width),
        ],
        axis=1,
    )
    key_grads = lax.psum_scatter(
        key_terms.astype(jnp.bfloat16), "seq", scatter_dimension=0, tiled=True
    ).astype(jnp.float32)
    grad_proj = jnp.concatenate(
        [grad_queries.reshape(owner_row_list, query_row_width), key_grads], axis=1
    ).astype(jnp.bfloat16)
    grad_cols = lax.all_to_all(grad_proj, "dp", split_axis=1, concat_axis=0, tiled=True)
    row_source = lax.all_gather(own_rows, "dp", axis=0, tiled=True)
    weight_grad = lax.psum_scatter(
        contract_rows(row_source, grad_cols).astype(jnp.bfloat16),
        "seq",
        scatter_dimension=0,
        tiled=True,
    ).astype(jnp.float32)
    grad_pooled = lax.psum_scatter(
        lax.dot_general(
            grad_cols, qkv_weight, (((1,), (1,)), ((), ())), preferred_element_type=jnp.float32
        ).astype(jnp.bfloat16),
        "dp",
        scatter_dimension=0,
        tiled=True,
    )
    back_rows = contract_rows(collect_low, grad_pooled).astype(jnp.bfloat16)
    returned = lax.all_to_all(
        back_rows.reshape(seq_count, capacity, -1), "seq", split_axis=0, concat_axis=0, tiled=True
    )
    slot_grads = contract_rows(routing_low, returned.reshape(seq_count * capacity, -1))
    scaled = slot_grads / jnp.maximum(counts, 1.0)[:, None]
    state_grad = lax.dot_general(
        onehot.astype(jnp.float32),
        scaled,
        (((0,), (0,)), ((), ())),
        precision=lax.Precision.HIGHEST,
        preferred_element_type=jnp.float32,
    ).astype(jnp.bfloat16)
    return (attn_rows[None], state_grad[None], weight_grad)


def solution(mesh):
    return jax.shard_map(
        body,
        mesh=mesh,
        in_specs=(
            P("dp", "seq", None),
            P("dp", "seq"),
            P("dp", None),
            P(None, "dp"),
            P("dp", "seq", None),
        ),
        out_specs=(P("dp", "seq", None), P("dp", "seq", None), P("seq", "dp")),
        check_vma=False,
    )
```

profile of v0, /device:TPU:0, one launch (start us, length us, event | category | flops | bytes accessed | tf_op | source)
XLA Modules:
  0.0 420.6 jit_solution(422287512734357633)
XLA Ops:
  7.2 1.3 slice.16
  8.5 1.3 broadcast_subtract_fusion
  11.1 0.7 reduce.1
  11.8 0.1 convert_reduce_fusion
  12.6 0.7 fusion.49
  13.3 0.1 fusion.37
  13.4 0.1 select_reduce_fusion
  13.6 0.7 add.60
  14.3 7.3 %all-to-all-start = ((s32[8,1,16]{2,1,0:T(1,128)}), s32[8,1,16]{2,1,0:T(1,128)S(1)}, u32[]{:S(2)}, u32[]{:S(2)}) async-start(s32[8,1,16]{2,1,0:T(1,128)} %bitcast.4), calls=%async_computation | async-start | bytes 8192 | tf_op jit(solution)/shard_map/all_to_all | solution.py:56
  21.6 1.7 convolution_convert_fusion.4
  23.3 4.7 %all-to-all-done = s32[8,1,16]{2,1,0:T(1,128)S(1)} async-done(((s32[8,1,16]{2,1,0:T(1,128)}), s32[8,1,16]{2,1,0:T(1,128)S(1)}, u32[]{:S(2)}, u32[]{:S(2)}) %all-to-all-start) | async-done | bytes 544 | tf_op jit(solution)/shard_map/all_to_all | solution.py:56
  28.0 3.6 all-to-all-start.1
  31.6 0.5 broadcast.120
  32.1 0.7 reduce.6
  32.9 23.4 %all-to-all-done.1 = bf16[8,16,4096]{2,1,0:T(8,128)(2,1)S(1)} async-done(((bf16[8,16,4096]{2,1,0:T(8,128)(2,1)}), bf16[8,16,4096]{2,1,0:T(8,128)(2,1)S(1)}, u32[]{:S(2)}, u32[]{:S(2)}) %all-to-all-start.1) | async-done | bytes 1048608 | tf_op jit(solution)/shard_map/all_to_all | solution.py:49
  56.3 1.1 convolution_convert_fusion.5
  57.5 23.0 %all-gather.3.cloned.1.call-done = bf16[288,4096]{1,0:T(8,128)(2,1)} async-done(((bf16[72,4096]{1,0:T(8,128)(2,1)}), bf16[288,4096]{1,0:T(8,128)(2,1)}) %all-gather.3.cloned.1.call-update) | async-done | bytes 2359312 | tf_op jit(solution)/shard_map/all_gather | solution.py:69
  80.5 5.5 %convolution_convert_fusion.6 = bf16[288,768]{1,0:T(8,128)(2,1)S(1)} fusion(bf16[288,4096]{1,0:T(8,128)(2,1)} %all-gather.3.cloned.1.call-done, bf16[4096,768]{1,0:T(8,128)(2,1)} %param.8), kind=kOutput, calls=%fused_computation.27 | convolution fusion | flops 1812160512 | bytes 9093120 | tf_op jit(solution)/shard_map/dot_general | solution.py:70
  86.0 10.4 %all_to_all.51 = bf16[4,72,768]{2,1,0:T(8,128)(2,1)S(1)} all-to-all(bf16[4,72,768]{2,1,0:T(8,128)(2,1)S(1)} %bitcast.113), channel_id=1, replica_groups=mesh['seq'=8,'dp'=4] {'dp'}, dimensions={0} | all-to-all | bytes 884736 | tf_op jit(solution)/shard_map/all_to_all | solution.py:73
  96.5 0.7 slice.21
  97.2 0.2 reshape_squeeze.3
  97.5 0.6 dynamic-slice
  98.7 0.1 select_reduce_fusion.1
  98.8 0.2 dynamic-update-slice
  99.1 11.5 %all-reduce.1 = s32[576]{0:T(1024)S(1)} all-reduce(s32[576]{0:T(1024)S(1)} %dynamic-update-slice), channel_id=1, replica_groups=mesh['seq'=8,'dp'=4] {'seq'}, use_global_device_ids=true, to_apply=%add.1 | all-reduce | flops 576 | bytes 4608
  110.6 0.7 slice.24
  111.4 1.1 reshape.214
  112.5 25.9 %all-gather.5.cloned.1.call-done = bf16[576,1024]{1,0:T(8,128)(2,1)} async-done(((bf16[72,1024]{1,0:T(8,128)(2,1)}), bf16[576,1024]{1,0:T(8,128)(2,1)}) %all-gather.5.cloned.1.call-update) | async-done | bytes 1179664 | tf_op jit(solution)/shard_map/all_gather | solution.py:82
  138.5 2.3 fusion.53
  140.8 1.6 reshape.213
  142.4 2.3 reshape.212
  144.7 0.7 fusion.22
  145.3 1.4 fusion.54
  146.7 0.3 fusion.18
  147.0 1.2 copy-done.3
  148.2 1.2 bitcast_convert_fusion
  149.4 1.6 fusion.15
  151.0 0.5 multiply_reduce_fusion
  151.5 0.1 copy.63
  151.6 2.8 fusion.4
  154.4 0.8 fusion.16
  155.2 0.1 copy.102
  155.3 0.6 copy-done.4
  155.9 0.1 copy.101
  156.0 1.2 pad_maximum_fusion
  157.2 0.2 reduce-scatter.6.cloned.1.call-start
  157.4 1.9 fusion.19
  159.3 0.1 copy.48
  159.4 0.2 reshape.215
  159.6 61.0 %reduce-scatter.4.cloned.1.call-done = bf16[72,1024]{1,0:T(8,128)(2,1)} async-done(((bf16[576,1024]{1,0:T(8,128)(2,1)}), bf16[72,1024]{1,0:T(8,128)(2,1)}) %reduce-scatter.4.cloned.1.call-update) | async-done | bytes 147472 | tf_op jit(solution)/shard_map/reduce_scatter | solution.py:133
  220.6 0.9 pad_maximum_fusion.1
  221.6 10.5 %all_to_all.52 = bf16[72,4,768]{2,0,1:T(8,128)(2,1)S(1)} all-to-all(bf16[72,4,768]{2,0,1:T(8,128)(2,1)S(1)} %bitcast.109), channel_id=1, replica_groups=mesh['seq'=8,'dp'=4] {'dp'}, dimensions={1} | all-to-all | bytes 884736 | tf_op jit(solution)/shard_map/all_to_all | solution.py:139
  232.1 6.3 %convolution_convert_fusion.1 = bf16[288,4096]{1,0:T(8,128)(2,1)} fusion(bf16[288,768]{1,0:T(8,128)(2,1)S(1)} %bitcast.111, bf16[4096,768]{1,0:T(8,128)(2,1)} %param.8), kind=kOutput, calls=%fused_computation.2 | convolution fusion | flops 1813118976 | bytes 9093120 | tf_op jit(solution)/shard_map/dot_general | solution.py:148
  238.5 7.8 %convolution_convert_fusion = bf16[4096,768]{1,0:T(8,128)(2,1)} fusion(bf16[288,4096]{1,0:T(8,128)(2,1)} %all-gather.3.cloned.1.call-done, bf16[288,768]{1,0:T(8,128)(2,1)S(1)} %bitcast.112), kind=kOutput, calls=%fused_computation.1 | convolution fusion | flops 1815085056 | bytes 9093120 | tf_op jit(solution)/shard_map/dot_general | solution.py:12
  246.3 23.2 %reduce-scatter.6.cloned.1.call-done = bf16[72,4096]{1,0:T(8,128)(2,1)} async-done(((bf16[288,4096]{1,0:T(8,128)(2,1)}), bf16[72,4096]{1,0:T(8,128)(2,1)}) %reduce-scatter.6.cloned.1.call-update) | async-done | bytes 589840 | tf_op jit(solution)/shard_map/reduce_scatter | solution.py:147
  269.5 2.5 convolution_convert_fusion.3
  272.0 5.5 %all-to-all-start.4 = ((bf16[8,16,4096]{2,1,0:T(8,128)(2,1)}), bf16[8,16,4096]{2,1,0:T(8,128)(2,1)}, u32[]{:S(2)}, u32[]{:S(2)}) async-start(bf16[8,16,4096]{2,1,0:T(8,128)(2,1)} %bitcast.28), calls=%async_computation.6 | async-start | bytes 2097152 | tf_op jit(solution)/shard_map/all_to_all | solution.py:156
  277.5 0.1 copy.44
  277.6 0.9 convert_element_type.81
  278.5 49.0 %all-to-all-done.4 = bf16[8,16,4096]{2,1,0:T(8,128)(2,1)} async-done(((bf16[8,16,4096]{2,1,0:T(8,128)(2,1)}), bf16[8,16,4096]{2,1,0:T(8,128)(2,1)}, u32[]{:S(2)}, u32[]{:S(2)}) %all-to-all-start.4) | async-done | bytes 1048608 | tf_op jit(solution)/shard_map/all_to_all | solution.py:156
  327.5 1.7 convolution_divide_fusion
  329.2 3.2 fusion.1
  332.4 79.2 %reduce-scatter.8.cloned.1.call-done = bf16[512,768]{1,0:T(8,128)(2,1)} async-done(((bf16[4096,768]{1,0:T(8,128)(2,1)}), bf16[512,768]{1,0:T(8,128)(2,1)}) %reduce-scatter.8.cloned.1.call-update) | async-done | bytes 786448 | tf_op jit(solution)/shard_map/reduce_scatter | solution.py:141
  411.6 2.4 convert_element_type.88
  (33 shorter events, 0.6 us)
Async XLA Ops:
  7.2 14.4 %copy-start = (bf16[1,256,4096]{2,1,0:T(8,128)(2,1)S(1)}, bf16[1,256,4096]{2,1,0:T(8,128)(2,1)}, u32[]{:S(2)}) copy-start(bf16[1,256,4096]{2,1,0:T(8,128)(2,1)} %param.5) | copy-start | bytes 6291460
  14.3 13.7 %all-to-all-start = ((s32[8,1,16]{2,1,0:T(1,128)}), s32[8,1,16]{2,1,0:T(1,128)S(1)}, u32[]{:S(2)}, u32[]{:S(2)}) async-start(s32[8,1,16]{2,1,0:T(1,128)} %bitcast.4), calls=%async_computation | async-start | bytes 8192 | tf_op jit(solution)/shard_map/all_to_all | solution.py:56
  28.0 28.3 %all-to-all-start.1 = ((bf16[8,16,4096]{2,1,0:T(8,128)(2,1)}), bf16[8,16,4096]{2,1,0:T(8,128)(2,1)S(1)}, u32[]{:S(2)}, u32[]{:S(2)}) async-start(bf16[8,16,4096]{2,1,0:T(8,128)(2,1)} %bitcast.110), calls=%async_computation.1 | async-start | bytes 2097152 | tf_op jit(solution)/shard_map/all_to_all | solution.py:49
  31.6 48.9 %all-gather.3.cloned.1.call-start = ((), (), s32[]{:S(2)}) async-start(), calls=%async_computation.8 | async-start | bytes 2949120 | tf_op jit(solution)/shard_map/all_gather | solution.py:69
  57.4 81.0 %all-gather.5.cloned.1.call-start = ((), (), s32[]{:S(2)}) async-start(), calls=%async_computation.9 | async-start | bytes 1327104 | tf_op jit(solution)/shard_map/all_gather | solution.py:82
  86.0 11.3 %copy-start.6 = (bf16[1,72,2048]{2,1,0:T(8,128)(2,1)S(1)}, bf16[1,72,2048]{2,1,0:T(8,128)(2,1)}, u32[]{:S(2)}) copy-start(bf16[1,72,2048]{2,1,0:T(8,128)(2,1)} %param.9) | copy-start | bytes 884740
  86.0 11.5 %copy-start.7 = (u32[32]{0:T(128)S(1)}, u32[32]{0:T(128)}, u32[]{:S(2)}) copy-start(u32[32]{0:T(128)} %constant.57) | copy-start | bytes 388
  97.2 123.5 %reduce-scatter.4.cloned.1.call-start = ((), (), s32[]{:S(2)}) async-start(), calls=%async_computation.10 | async-start | bytes 1327104 | tf_op jit(solution)/shard_map/reduce_scatter | solution.py:133
  146.7 2.7 copy-start.2
  146.7 1.5 copy-start.3
  154.4 1.6 copy-start.1
  154.4 1.5 copy-start.4
  157.2 112.3 %reduce-scatter.6.cloned.1.call-start = ((), (), s32[]{:S(2)}) async-start(), calls=%async_computation.11 | async-start | bytes 2949120 | tf_op jit(solution)/shard_map/reduce_scatter | solution.py:147
  238.4 173.2 %reduce-scatter.8.cloned.1.call-start = ((), (), s32[]{:S(2)}) async-start(), calls=%async_computation.12 | async-start | bytes 7077888 | tf_op jit(solution)/shard_map/reduce_scatter | solution.py:141
  246.3 31.2 %copy-start.5 = (bf16[72,4,4,128]{3,0,2,1:T(8,128)(2,1)S(1)}, bf16[72,4,4,128]{3,0,2,1:T(8,128)(2,1)}, u32[]{:S(2)}) copy-start(bf16[72,4,4,128]{3,0,2,1:T(8,128)(2,1)} %get-tuple-element.7) | copy-start | bytes 884740
  272.0 55.5 %all-to-all-start.4 = ((bf16[8,16,4096]{2,1,0:T(8,128)(2,1)}), bf16[8,16,4096]{2,1,0:T(8,128)(2,1)}, u32[]{:S(2)}, u32[]{:S(2)}) async-start(bf16[8,16,4096]{2,1,0:T(8,128)(2,1)} %bitcast.28), calls=%async_computation.6 | async-start | bytes 2097152 | tf_op jit(solution)/shard_map/all_to_all | solution.py:156
Sparse Core Ops, SparseCore 0:
  57.6 22.8 all-gather.2
  97.3 41.1 all-gather.4
  157.3 63.3 reduce-scatter.3
  238.5 30.8 reduce-scatter.5
  272.9 138.6 reduce-scatter.7
where the time goes:
time: 421 us
  waiting for transfers between devices  289 us (69%)
  matrix products  38.8 us (9%)
  blocking collectives  32.4 us (8%)
  starting transfers between devices  16.7 us (4%)
  between operations  16.7 us (4%)
  local copies, waits for them, and re-layouts  15.9 us (4%)
  other arithmetic  10.6 us (3%)
    reduce_scatter x1, waiting for transfers between devices, body(): lax.psum_scatter(contract_rows(row_source, grad_cols).astype(jnp.bfloat16...  79.2 us
    reduce_scatter x1, waiting for transfers between devices, body(): lax.psum_scatter(key_terms.astype(jnp.bfloat16), 'seq', scatter_dimension...  61 us
    all_to_all x1, waiting for transfers between devices, body(): lax.all_to_all(back_rows.reshape(seq_count, capacity, -1), 'seq', split_a...  49 us
    all_gather x1, waiting for transfers between devices, body(): lax.all_gather(key_value, 'seq', axis=0, tiled=True)  25.9 us
    all_to_all x1, waiting for transfers between devices, body(): lax.all_to_all(send_rows.reshape(seq_count, capacity, -1), 'seq', split_a...  23.4 us
    reduce_scatter x1, waiting for transfers between devices, body(): lax.psum_scatter(lax.dot_general(grad_cols, qkv_weight, (((1,), (1,)), ((...  23.2 us
    all_gather x1, waiting for transfers between devices, body(): all_rows = lax.all_gather(own_rows, 'dp', axis=0, tiled=True)  23 us
    dot_general x3, matrix products, contract_rows(): lax.dot_general(left, right, (((0,), (0,)), ((), ())), preferred_element_...  12 us
  transfers between devices with their start and end apart: 8, of which 8 were waited for; matrix products, arithmetic and copies ran while one was open for 6% of the time, Pallas kernels for 0%

commit v1 on v0

v1 whole, which is shorter than its diff:
```python
import functools

import jax
import jax.numpy as jnp
from jax import lax
from jax.experimental import pallas as pl
from jax.experimental.pallas import tpu as pltpu
from jax.sharding import PartitionSpec as P

QUERY_HEADS = 16
KEY_VALUE_HEADS = 4
HEAD_SIZE = 128
BF = jnp.bfloat16
F32 = jnp.float32


def dot(left, right, dims):
    return lax.dot_general(left, right, (dims, ((), ())), preferred_element_type=F32)


def attention_kernel(
    n, base, extra, heads, splits, block,
    spike_ref, unit_ref, target_ref, qkv_ref, cot_ref, out_ref, grad_ref,
    cot_scratch, out_scratch, key_scratch, value_scratch,
):
    rows = base + extra
    total = qkv_ref.shape[0]
    width = heads * HEAD_SIZE
    factor = HEAD_SIZE ** (-0.5)
    spike = spike_ref[0]

    def patch_of(position):
        holder = jnp.zeros_like(position)
        for k in range(1, n):
            holder = holder + (position >= k * rows).astype(jnp.int32)
        slot = position - holder * rows
        plain = base * (holder + (holder > spike).astype(jnp.int32)) + slot
        spread = base * (spike + 1) + holder * extra + (slot - base)
        return jnp.where(slot < base, plain, spread)

    lanes = lax.broadcasted_iota(jnp.int32, (1, total), 1)
    patch_row = patch_of(lanes)

    for start in range(0, total, block):
        pick = (target_ref[start : start + block, :] == lanes).astype(BF)
        cot_scratch[start : start + block, :] = dot(
            pick, cot_ref[...], ((1,), (0,))
        ).astype(BF)

    keys = qkv_ref[:, width : width + HEAD_SIZE]
    values = qkv_ref[:, width + HEAD_SIZE : width + 2 * HEAD_SIZE]
    for start in range(0, total, block):
        stop = start + block
        position = start + lax.broadcasted_iota(jnp.int32, (block, 1), 0)
        patch_col = patch_of(position)
        allowed = patch_row <= patch_col
        pick = (patch_col == lanes).astype(BF)
        cot = dot(pick, cot_scratch[...], ((1,), (0,))).astype(BF)
        outs = []
        for head in range(heads):
            cols = slice(head * HEAD_SIZE, (head + 1) * HEAD_SIZE)
            query = qkv_ref[start:stop, cols]
            scores = dot(query, keys, ((1,), (1,))) * factor
            scores = jnp.where(allowed, scores, -jnp.inf)
            peak = jnp.max(scores, axis=-1, keepdims=True)
            shifted = jnp.exp(scores - peak)
            attend = shifted / jnp.sum(shifted, axis=-1, keepdims=True)
            if splits > 1:
                part = (position * splits) // total
                attend = jnp.where(part == unit_ref[0] % splits, attend, 0.0)
            low = attend.astype(BF)
            attended = dot(low, values, ((1,), (0,)))
            outs.append(attended.astype(BF))
            cot_head = cot[:, cols]
            grad_attend = dot(cot_head, values, ((1,), (1,)))
            delta = jnp.sum(cot_head.astype(F32) * attended, axis=-1, keepdims=True)
            score_grad = (attend * (grad_attend - delta)).astype(BF)
            grad_ref[start:stop, cols] = (
                dot(score_grad, keys, ((1,), (0,))) * factor
            ).astype(BF)
            key_term = dot(score_grad, query, ((0,), (0,)))
            value_term = dot(low, cot_head, ((0,), (0,)))
            if start == 0 and head == 0:
                key_scratch[...] = key_term
                value_scratch[...] = value_term
            else:
                key_scratch[...] += key_term
                value_scratch[...] += value_term
        term = dot(pick, jnp.concatenate(outs, axis=1), ((0,), (0,)))
        if start == 0:
            out_scratch[...] = term
        else:
            out_scratch[...] += term
    grad_ref[:, width : width + HEAD_SIZE] = (key_scratch[...] * factor).astype(BF)
    grad_ref[:, width + HEAD_SIZE :] = value_scratch[...].astype(BF)
    placed = out_scratch[...].astype(BF)
    for start in range(0, total, block):
        pick = (target_ref[start : start + block, :] == lanes).astype(BF)
        term = dot(pick, placed[start : start + block, :], ((0,), (0,)))
        if start == 0:
            out_scratch[...] = term
        else:
            out_scratch[...] += term
    out_ref[...] = out_scratch[...].astype(BF)


def attention_call(n, base, extra, heads, splits, spike, unit, target, qkv, cot):
    total, wide = qkv.shape
    width = heads * HEAD_SIZE
    block = max(b for b in range(16, 193, 16) if total % b == 0)
    vmem = pl.BlockSpec(memory_space=pltpu.VMEM)
    smem = pl.BlockSpec(memory_space=pltpu.SMEM)
    return pl.pallas_call(
        functools.partial(attention_kernel, n, base, extra, heads, splits, block),
        out_shape=(
            jax.ShapeDtypeStruct((total, width), BF),
            jax.ShapeDtypeStruct((total, wide), BF),
        ),
        in_specs=[smem, smem, vmem, vmem, vmem],
        out_specs=(vmem, vmem),
        scratch_shapes=[
            pltpu.VMEM((total, width), BF),
            pltpu.VMEM((total, width), F32),
            pltpu.VMEM((total, HEAD_SIZE), F32),
            pltpu.VMEM((total, HEAD_SIZE), F32),
        ],
        compiler_params=pltpu.CompilerParams(vmem_limit_bytes=48 * 1024 * 1024),
        name="attention",
    )(spike, unit, target, qkv, cot)


def body(byte_states, byte_patch, patch_owner, qkv_weight, attention_output_gradient):
    n, nd = lax.axis_size("seq"), lax.axis_size("dp")
    nx = nd // 2
    column_index = lax.axis_index("dp")
    seq_index = lax.axis_index("seq")
    ny = 1
    while 2 * (2 * ny) ** 2 <= n:
        ny *= 2
    nz = n // ny

    byte_rows = byte_states[0]
    byte_total, model = byte_rows.shape
    slot_count = byte_total // 2
    base = byte_total // 4
    owner_rows = attention_output_gradient.shape[1]
    extra = owner_rows - base
    total = patch_owner.shape[1]
    columns = qkv_weight.shape[1]

    def dp_hop(value, distance):
        return lax.ppermute(value, "dp", [(i, i ^ distance) for i in range(nd)])

    def seq_swap(value):
        return lax.all_to_all(value, "seq", split_axis=0, concat_axis=0, tiled=True)

    def dp_gather(value):
        blocks = [None] * nd
        blocks[0] = value
        for k in range(1, nx):
            blocks[2 * k] = dp_hop(value, 2 * k)
        for k in range(nx):
            blocks[2 * k + 1] = dp_hop(blocks[2 * k], 1)
        return blocks

    def dp_swap(blocks):
        across = [None] * nx
        across[0] = (blocks[0], blocks[1])
        for k in range(1, nx):
            got = dp_hop(jnp.stack([blocks[2 * k], blocks[2 * k + 1]]), 2 * k)
            across[k] = (got[0], got[1])
        result = [None] * nd
        first = dp_hop(across[0][1], 1)
        rest = dp_hop(jnp.stack([across[k][1] for k in range(1, nx)]), 1)
        for k in range(nx):
            result[2 * k] = across[k][0]
            result[2 * k + 1] = first if k == 0 else rest[k - 1]
        return result

    def dp_reduce(value):
        pairs = value.reshape((nx, 2) + value.shape[1:])
        got = dp_hop(pairs[:, 1], 1)
        held = (pairs[:, 0].astype(F32) + got.astype(F32)).astype(BF)
        result = held[0].astype(F32)
        for k in range(1, nx):
            result = result + dp_hop(held[k], 2 * k).astype(F32)
        return result.astype(BF)

    patch_ids = byte_patch[0]
    first_patch = patch_ids[0]
    local_ids = patch_ids - first_patch
    slot_range = jnp.arange(slot_count, dtype=jnp.int32)
    onehot = local_ids[None, :] == slot_range[:, None]
    counts = jnp.sum(onehot.astype(F32), axis=1)
    summed = dot(onehot.astype(BF), byte_rows, ((1,), (0,)))
    pooled = (summed / jnp.maximum(counts, 1.0)[:, None]).astype(BF)
    base_rows = pooled[:base]
    spread = seq_swap(pooled[base:].reshape(n, extra, model))
    extra_rows = jnp.sum(spread.astype(F32), axis=0).astype(BF)

    base_all = jnp.concatenate(dp_gather(base_rows), axis=0)
    extra_all = jnp.concatenate(dp_gather(extra_rows), axis=0)
    proj_base = dot(base_all, qkv_weight, ((1,), (0,))).astype(BF).reshape(nd, base, columns)
    proj_extra = dot(extra_all, qkv_weight, ((1,), (0,))).astype(BF).reshape(nd, extra, columns)
    proj = jnp.concatenate([proj_base, proj_extra], axis=1)

    relative = jnp.stack(dp_swap([proj[r] for r in range(nd)]))
    projected = jnp.concatenate(
        [
            lax.dynamic_index_in_dim(relative, column_index ^ k, 0, keepdims=False)
            for k in range(nd)
        ],
        axis=1,
    )

    heads = max(1, QUERY_HEADS // n)
    splits = max(1, n // QUERY_HEADS)
    width = heads * HEAD_SIZE
    query_width = QUERY_HEADS * HEAD_SIZE
    key_width = KEY_VALUE_HEADS * HEAD_SIZE
    group = QUERY_HEADS // KEY_VALUE_HEADS

    def query_of(unit):
        return (unit // splits) * width

    def key_of(unit):
        return query_width + (unit // splits) * heads // group * HEAD_SIZE

    sends = []
    for unit in range(n):
        q, k = query_of(unit), key_of(unit)
        sends.append(
            jnp.concatenate(
                [
                    projected[:, q : q + width],
                    projected[:, k : k + HEAD_SIZE],
                    projected[:, k + key_width : k + key_width + HEAD_SIZE],
                ],
                axis=1,
            )
        )
    qkv = seq_swap(jnp.stack(sends)).reshape(total, width + 2 * HEAD_SIZE)

    cotangent = attention_output_gradient[0]
    behind = (first_patch // base - seq_index).astype(BF)
    flags = jnp.broadcast_to(behind, (n, 8, width))
    cot_sends = jnp.stack(
        [cotangent[:, query_of(unit) : query_of(unit) + width] for unit in range(n)]
    )
    cot_got = seq_swap(jnp.concatenate([cot_sends, flags], axis=1))
    cot = cot_got[:, :owner_rows].reshape(total, width)
    after = jnp.sum(cot_got[:, owner_rows, 0].astype(F32)).astype(jnp.int32)
    spike = n - 1 - after

    patch_range = jnp.arange(total, dtype=jnp.int32)
    target = (patch_owner[0] * owner_rows + patch_range // n)[:, None]
    out_rows, grads = attention_call(
        n, base, extra, heads, splits,
        spike.reshape(1), seq_index.astype(jnp.int32).reshape(1), target, qkv, cot,
    )

    out_got = seq_swap(out_rows.reshape(n, owner_rows, width))
    if splits > 1:
        out_got = jnp.sum(
            out_got.astype(F32).reshape(n // splits, splits, owner_rows, width), axis=1
        ).astype(BF)
    attn = jnp.concatenate([out_got[u] for u in range(n // splits)], axis=1)

    grads_got = seq_swap(grads.reshape(n, owner_rows, width + 2 * HEAD_SIZE))
    pieces = []
    for unit in range(0, n, splits):
        piece = grads_got[unit, :, :width]
        if splits > 1:
            piece = jnp.sum(
                grads_got[unit : unit + splits, :, :width].astype(F32), axis=0
            ).astype(BF)
        pieces.append(piece)
    per_key = n // KEY_VALUE_HEADS
    for offset in (width, width + HEAD_SIZE):
        for head in range(KEY_VALUE_HEADS):
            part = grads_got[
                head * per_key : (head + 1) * per_key, :, offset : offset + HEAD_SIZE
            ]
            pieces.append(jnp.sum(part.astype(F32), axis=0).astype(BF))
    grad_proj = jnp.concatenate(pieces, axis=1)
    grad_blocks = jnp.stack(
        [grad_proj[:, k * columns : (k + 1) * columns] for k in range(nd)]
    )
    grad_cols = jnp.stack(
        dp_swap(
            [
                lax.dynamic_index_in_dim(grad_blocks, column_index ^ r, 0, keepdims=False)
                for r in range(nd)
            ]
        )
    )

    back_extra = dot(
        grad_cols[:, base:].reshape(nd * extra, columns), qkv_weight, ((1,), (1,))
    ).astype(BF)
    extra_grad = dp_reduce(back_extra.reshape(nd, extra, model))
    to_spike = (jnp.arange(n, dtype=jnp.int32) == spike)[:, None, None]
    extra_back = seq_swap(jnp.where(to_spike, extra_grad[None], jnp.zeros((), BF)))
    back_base = dot(
        grad_cols[:, :base].reshape(nd * base, columns), qkv_weight, ((1,), (1,))
    ).astype(BF)
    base_grad = dp_reduce(back_base.reshape(nd, base, model))
    slot_grads = jnp.concatenate([base_grad, extra_back.reshape(base, model)], axis=0)
    byte_counts = jnp.sum(jnp.where(onehot, counts[:, None], 0.0), axis=0)
    picked = dot(onehot.astype(BF), slot_grads, ((0,), (0,)))
    state_grad = (picked / jnp.maximum(byte_counts, 1.0)[:, None]).astype(BF)

    own_rows = jnp.concatenate([base_rows, extra_rows], axis=0)
    strip = model // n
    strips = seq_swap(
        jnp.stack([own_rows[:, k * strip : (k + 1) * strip] for k in range(n)])
    )
    all_strips = jnp.stack(dp_gather(strips), axis=1)
    zi, yi = seq_index // ny, seq_index % ny
    current = grad_cols.reshape(nd * owner_rows, columns)
    weight_grad = jnp.zeros((strip, columns), F32)
    for kz in range(nz):
        for ky in range(ny):
            moved = current
            if ky:
                moved = lax.ppermute(
                    current,
                    "seq",
                    [(z * ny + y, z * ny + (y + ky) % ny) for z in range(nz) for y in range(ny)],
                )
            source = ((zi - kz) % nz) * ny + (yi - ky) % ny
            left = lax.dynamic_index_in_dim(all_strips, source, 0, keepdims=False)
            weight_grad = weight_grad + dot(
                left.reshape(nd * owner_rows, strip), moved, ((0,), (0,))
            )
        if kz < nz - 1:
            current = lax.ppermute(
                current,
                "seq",
                [(z * ny + y, ((z + 1) % nz) * ny + y) for z in range(nz) for y in range(ny)],
            )
    return (attn[None], state_grad[None], weight_grad)


def solution(mesh):
    return jax.shard_map(
        body,
        mesh=mesh,
        in_specs=(
            P("dp", "seq", None),
            P("dp", "seq"),
            P("dp", None),
            P(None, "dp"),
            P("dp", "seq", None),
        ),
        out_specs=(P("dp", "seq", None), P("dp", "seq", None), P("seq", "dp")),
        check_vma=False,
    )
```

time: 421 us -> 215 us (0.51)
  waiting for transfers between devices: 289 us -> 82.2 us
  blocking collectives: 32.4 us -> 0 us
  starting transfers between devices: 16.7 us -> 47.7 us
  between operations: 16.7 us -> 4.56 us
  local copies, waits for them, and re-layouts: 15.9 us -> 24.7 us
  matrix products: 38.8 us -> 31.3 us
  Pallas kernels: 0 us -> 7.15 us
  other arithmetic: 10.6 us -> 15.4 us
    reduce_scatter x3 -> x0, waiting for transfers between devices: 163 us -> none  [the longest x1 79.2 us: body(): lax.psum_scatter(contract_rows(row_source, grad_cols).astype(jnp.bfloat16...]
    all_gather x2 -> x0, waiting for transfers between devices: 48.9 us -> none  [the longest x1 25.9 us: body(): lax.all_gather(key_value, 'seq', axis=0, tiled=True)]
    ppermute x0 -> x26, waiting for transfers between devices: none -> 36.6 us  [the longest x19 18.5 us: dp_hop(): return lax.ppermute(value, 'dp', [(i, i ^ distance) for i in range(nd)])]
    all_to_all x3 -> x7, waiting for transfers between devices: 77.1 us -> 45.6 us  [seq_swap(): return lax.all_to_all(value, 'seq', split_axis=0, concat_axis=0, tiled=True)]
    all_to_all x2 -> x0, blocking collectives: 20.9 us -> none  [the longest x1 10.5 us: body(): lax.all_to_all(grad_proj, 'dp', split_axis=1, concat_axis=0, tiled=True)]
    ppermute x0 -> x26, starting transfers between devices: none -> 16.2 us  [the longest x19 8.03 us: dp_hop(): return lax.ppermute(value, 'dp', [(i, i ^ distance) for i in range(nd)])]
    all_to_all x3 -> x7, starting transfers between devices: 16.4 us -> 31.5 us  [seq_swap(): return lax.all_to_all(value, 'seq', split_axis=0, concat_axis=0, tiled=True)]
    unnamed x1 -> x0, blocking collectives: 11.5 us -> none
  transfers between devices with their start and end apart: 8 -> 33, of which waited for: 8 -> 14; matrix products, arithmetic and copies ran while one was open for 6% -> 28% of each run, Pallas kernels for 0% -> 3%
where the time goes in v1:
time: 215 us; the launch traced here: 213 us
  waiting for transfers between devices  82.2 us (38%)
  starting transfers between devices  47.7 us (22%)
  matrix products  31.3 us (15%)
  local copies, waits for them, and re-layouts  24.7 us (11%)
  other arithmetic  15.4 us (7%)
  Pallas kernels  7.15 us (3%)
  between operations  4.56 us (2%)
    all_to_all x7, waiting for transfers between devices, seq_swap(): return lax.all_to_all(value, 'seq', split_axis=0, concat_axis=0, tiled=True)  45.6 us
    all_to_all x7, starting transfers between devices, seq_swap(): return lax.all_to_all(value, 'seq', split_axis=0, concat_axis=0, tiled=True)  31.5 us
    dot_general x14, matrix products, dot(): lax.dot_general(left, right, (dims, ((), ())), preferred_element_type=F32)  31.3 us
    ppermute x19, waiting for transfers between devices, dp_hop(): return lax.ppermute(value, 'dp', [(i, i ^ distance) for i in range(nd)])  18.5 us
    ppermute x3, waiting for transfers between devices, body(): lax.ppermute(current, 'seq', [(z * ny + y, (z + 1) % nz * ny + y) for z i...  18 us
    unnamed x69, local copies, waits for them, and re-layouts  14 us
    ppermute x19, starting transfers between devices, dp_hop(): return lax.ppermute(value, 'dp', [(i, i ^ distance) for i in range(nd)])  8.03 us
    pallas_call x1, Pallas kernels, attention_call(): pl.pallas_call(functools.partial(attention_kernel, n, base, extra, heads,...  7.15 us
  transfers between devices with their start and end apart: 33, of which 14 were waited for; matrix products, arithmetic and copies ran while one was open for 28% of the time, Pallas kernels for 3%

profile of v1, /device:TPU:0, one launch (start us, length us, event | category | flops | bytes accessed | tf_op | source)
XLA Modules:
  0.0 213.1 jit_solution(5819992672526494948)
XLA Ops:
  0.6 1.3 slice.259
  2.0 1.3 broadcast_subtract_fusion
  3.9 0.9 fusion.62
  4.8 3.0 %collective-permute-start.1 = (bf16[64,4096]{1,0:T(8,128)(2,1)S(1)}, bf16[64,4096]{1,0:T(8,128)(2,1)}, u32[]{:S(2)}, u32[]{:S(2)}) collective-permute-start(bf16[64,4096]{1,0:T(8,128)(2,1)S(1)} %get-tuple-element.23), channel_id=1, source_target_pairs={{0,2},{1,3},{2,0},{3,1},{4,6},{5,7},{6,4},{7,5},{8,10},{9,11},{10,... | collective-permute-start | bytes 1572872 | tf_op jit(solution)/shard_map/ppermute | solution.py:152
  7.7 5.8 %all-to-all-start.1 = ((bf16[8,8,4096]{2,1,0:T(8,128)(2,1)}), bf16[8,8,4096]{2,1,0:T(8,128)(2,1)S(1)}, u32[]{:S(2)}, u32[]{:S(2)}) async-start(bf16[8,8,4096]{2,1,0:T(8,128)(2,1)} %get-tuple-element.24), calls=%async_computation.1 | async-start | bytes 1048576 | tf_op jit(solution)/shard_map/all_to_all | solution.py:155
  13.6 0.8 constant_dynamic-update-slice_fusion.7
  14.3 0.8 constant_dynamic-update-slice_fusion.6
  15.1 0.8 constant_dynamic-update-slice_fusion.5
  15.9 0.8 constant_dynamic-update-slice_fusion.4
  16.6 0.8 constant_dynamic-update-slice_fusion.3
  20.8 0.8 constant_dynamic-update-slice_fusion.1
  21.6 0.8 constant_dynamic-update-slice_fusion
  23.3 5.4 %all-to-all-done.1 = bf16[8,8,4096]{2,1,0:T(8,128)(2,1)S(1)} async-done(((bf16[8,8,4096]{2,1,0:T(8,128)(2,1)}), bf16[8,8,4096]{2,1,0:T(8,128)(2,1)S(1)}, u32[]{:S(2)}, u32[]{:S(2)}) %all-to-all-start.1) | async-done | bytes 524320 | tf_op jit(solution)/shard_map/all_to_all | solution.py:155
  28.7 3.6 %all-to-all-start = ((bf16[8,80,256]{2,1,0:T(8,128)(2,1)}), bf16[8,80,256]{2,1,0:T(8,128)(2,1)S(1)}, u32[]{:S(2)}, u32[]{:S(2)}) async-start(bf16[8,80,256]{2,1,0:T(8,128)(2,1)} %concatenate.58), calls=%async_computation | async-start | bytes 655360 | tf_op jit(solution)/shard_map/all_to_all | solution.py:155
  33.1 3.6 %collective-permute-done.4 = bf16[8,4096]{1,0:T(8,128)(2,1)S(1)} collective-permute-done((bf16[8,4096]{1,0:T(8,128)(2,1)S(1)}, bf16[8,4096]{1,0:T(8,128)(2,1)S(1)}, u32[]{:S(2)}, u32[]{:S(2)}) %collective-permute-start.4) | collective-permute-done | bytes 65568 | tf_op jit(solution)/shard_map/ppermute | solution.py:152
  36.8 5.1 %fusion.13 = bf16[256,768]{1,0:T(8,128)(2,1)S(1)} fusion(bf16[4096,768]{1,0:T(8,128)(2,1)} %param.8, bf16[64,4096]{1,0:T(8,128)(2,1)} %collective-permute-done.2, bf16[64,4096]{1,0:T(8,128)(2,1)} %collective-permute-done.1, bf16[64,4096]{1,0:T(8,128)(2,1)} %collective-permute-done, bf16[64,4096]{1,0:T(8,128)(2,1)S(1)} %get-tuple-element.23), kind=kOutput, calls=%fused_computation.27 | convolution fusion | flops 1619197952 | bytes 8781824 | tf_op jit(solution)/shard_map/dot_general | solution.py:18
  41.9 1.1 fusion.16
  44.0 7.0 %collective-permute-done.7 = bf16[2,72,768]{2,1,0:T(8,128)(2,1)S(1)} collective-permute-done((bf16[2,72,768]{2,1,0:T(8,128)(2,1)S(1)}, bf16[2,72,768]{2,1,0:T(8,128)(2,1)S(1)}, u32[]{:S(2)}, u32[]{:S(2)}) %collective-permute-start.7) | collective-permute-done | bytes 221216 | tf_op jit(solution)/shard_map/ppermute | solution.py:152
  51.1 1.3 collective-permute-done.8
  53.2 6.0 %all-to-all-start.6 = ((bf16[8,72,512]{2,1,0:T(8,128)(2,1)}), bf16[8,72,512]{2,1,0:T(8,128)(2,1)S(1)}, u32[]{:S(2)}, u32[]{:S(2)}) async-start(bf16[8,72,512]{2,1,0:T(8,128)(2,1)} %copy-done.19), calls=%async_computation.6 | async-start | bytes 1179648 | tf_op jit(solution)/shard_map/all_to_all | solution.py:155
  59.2 1.4 constant_dynamic-update-slice_fusion.15
  60.6 1.4 constant_dynamic-update-slice_fusion.14
  62.0 1.4 constant_dynamic-update-slice_fusion.13
  66.6 8.8 %all-to-all-done.6 = bf16[8,72,512]{2,1,0:T(8,128)(2,1)S(1)} async-done(((bf16[8,72,512]{2,1,0:T(8,128)(2,1)}), bf16[8,72,512]{2,1,0:T(8,128)(2,1)S(1)}, u32[]{:S(2)}, u32[]{:S(2)}) %all-to-all-start.6) | async-done | bytes 589856 | tf_op jit(solution)/shard_map/all_to_all | solution.py:155
  75.4 0.8 copy-done.10
  76.2 3.6 %all-to-all-start.2 = ((bf16[8,72,512]{2,1,0:T(8,128)(2,1)}), bf16[8,72,512]{2,1,0:T(8,128)(2,1)S(1)}, u32[]{:S(2)}, u32[]{:S(2)}) async-start(bf16[8,72,512]{2,1,0:T(8,128)(2,1)} %constant_dynamic-update-slice_fusion.8), calls=%async_computation.2 | async-start | bytes 1179648 | tf_op jit(solution)/shard_map/all_to_all | solution.py:155
  79.9 0.9 copy.13
  80.7 1.0 fusion.27.target_ref
  83.6 1.0 slice.357
  84.6 11.3 %all-to-all-done.2 = bf16[8,72,512]{2,1,0:T(8,128)(2,1)S(1)} async-done(((bf16[8,72,512]{2,1,0:T(8,128)(2,1)}), bf16[8,72,512]{2,1,0:T(8,128)(2,1)S(1)}, u32[]{:S(2)}, u32[]{:S(2)}) %all-to-all-start.2) | async-done | bytes 589856 | tf_op jit(solution)/shard_map/all_to_all | solution.py:155
  95.9 7.2 %attention.1 = (bf16[576,256]{1,0:T(8,128)(2,1)S(1)}, bf16[576,512]{1,0:T(8,128)(2,1)S(1)}) custom-call(s32[1]{0:T(128)} %bitcast.10.spike_ref, s32[1]{0:T(128)} %bitcast.11.unit_ref, s32[576,1]{1,0:T(8,128)S(1)} %fusion.27.target_ref, bf16[576,512]{1,0:T(8,128)(2,1)S(1)} %bitcast.246, bf16[576,256]{1,0:T(8,128)(2,1)S(1)} %bitcast.247), custom_call_target="tpu_custom_call" | custom-call | tf_op jit(solution)/shard_map/attention/pallas_call | solution.py:113
  103.1 0.8 copy-done.1
  104.6 3.6 %all-to-all-start.3 = ((bf16[8,72,256]{2,1,0:T(8,128)(2,1)}), bf16[8,72,256]{2,1,0:T(8,128)(2,1)S(1)}, u32[]{:S(2)}, u32[]{:S(2)}) async-start(bf16[8,72,256]{2,1,0:T(8,128)(2,1)} %bitcast.249), calls=%async_computation.3 | async-start | bytes 589824 | tf_op jit(solution)/shard_map/all_to_all | solution.py:155
  108.9 9.1 %all-to-all-done.3 = bf16[8,72,256]{2,1,0:T(8,128)(2,1)S(1)} async-done(((bf16[8,72,256]{2,1,0:T(8,128)(2,1)}), bf16[8,72,256]{2,1,0:T(8,128)(2,1)S(1)}, u32[]{:S(2)}, u32[]{:S(2)}) %all-to-all-start.3) | async-done | bytes 294944 | tf_op jit(solution)/shard_map/all_to_all | solution.py:155
  118.0 3.7 %all-to-all-start.4 = ((bf16[8,72,512]{2,1,0:T(8,128)(2,1)}), bf16[8,72,512]{2,1,0:T(8,128)(2,1)S(1)}, u32[]{:S(2)}, u32[]{:S(2)}) async-start(bf16[8,72,512]{2,1,0:T(8,128)(2,1)} %bitcast.248), calls=%async_computation.4 | async-start | bytes 1179648 | tf_op jit(solution)/shard_map/all_to_all | solution.py:155
  126.1 11.1 %all-to-all-done.4 = bf16[8,72,512]{2,1,0:T(8,128)(2,1)S(1)} async-done(((bf16[8,72,512]{2,1,0:T(8,128)(2,1)}), bf16[8,72,512]{2,1,0:T(8,128)(2,1)S(1)}, u32[]{:S(2)}, u32[]{:S(2)}) %all-to-all-start.4) | async-done | bytes 589856 | tf_op jit(solution)/shard_map/all_to_all | solution.py:155
  138.2 1.8 constant_dynamic-update-slice_fusion.16
  139.9 1.9 pad_maximum_fusion
  141.9 1.7 collective-permute-done.10
  143.7 1.2 constant_dynamic-slice_fusion
  145.0 2.0 collective-permute-start.19
  147.1 1.9 convolution_convert_fusion.1
  149.0 1.8 convolution_convert_fusion
  151.1 1.3 slice_bitcast_fusion
  153.0 1.8 fusion.70
  154.8 2.0 collective-permute-done.15
  156.8 0.9 broadcast_select_fusion
  157.7 5.0 %all-to-all-start.5 = ((bf16[8,8,4096]{2,1,0:T(8,128)(2,1)}), bf16[8,8,4096]{2,1,0:T(8,128)(2,1)}, u32[]{:S(2)}, u32[]{:S(2)}) async-start(bf16[8,8,4096]{2,1,0:T(8,128)(2,1)} %broadcast_select_fusion), calls=%async_computation.5 | async-start | bytes 1048576 | tf_op jit(solution)/shard_map/all_to_all | solution.py:155
  162.7 2.1 collective-permute-start.21
  164.8 1.5 collective-permute-start.22
  166.3 2.9 %fusion.72 = f32[512,768]{1,0:T(8,128)} fusion(bf16[288,512]{1,0:T(8,128)(2,1)} %bitcast.269, bf16[288,768]{1,0:T(8,128)(2,1)} %collective-permute-done.20), kind=kOutput, calls=%fused_computation.231 | convolution fusion | flops 226492416 | bytes 2310144 | tf_op jit(solution)/shard_map/dot_general | solution.py:18
  169.2 2.8 %fusion.71 = f32[512,768]{1,0:T(8,128)} fusion(bf16[288,512]{1,0:T(8,128)(2,1)S(1)} %bitcast.268, bf16[288,768]{1,0:T(8,128)(2,1)} %collective-permute-done.19), kind=kOutput, calls=%fused_computation.230 | convolution fusion | flops 226492416 | bytes 2310144 | tf_op jit(solution)/shard_map/dot_general | solution.py:18
  172.0 12.4 %collective-permute-done.22 = bf16[288,768]{1,0:T(8,128)(2,1)S(1)} collective-permute-done((bf16[288,768]{1,0:T(8,128)(2,1)}, bf16[288,768]{1,0:T(8,128)(2,1)S(1)}, u32[]{:S(2)}, u32[]{:S(2)}) %collective-permute-start.22) | collective-permute-done | bytes 442400 | tf_op jit(solution)/shard_map/ppermute | solution.py:337
  184.4 1.5 collective-permute-start.23
  186.6 1.8 fusion.74
  188.4 1.8 fusion.73
  190.1 1.5 fusion.11
  192.3 5.6 %collective-permute-done.24 = bf16[288,768]{1,0:T(8,128)(2,1)S(1)} collective-permute-done((bf16[288,768]{1,0:T(8,128)(2,1)S(1)}, bf16[288,768]{1,0:T(8,128)(2,1)S(1)}, u32[]{:S(2)}, u32[]{:S(2)}) %collective-permute-start.24) | collective-permute-done | bytes 442400 | tf_op jit(solution)/shard_map/ppermute | solution.py:337
  198.4 1.7 fusion.76
  200.1 1.8 fusion.75
  201.9 2.9 %collective-permute-done.13 = bf16[64,4096]{1,0:T(8,128)(2,1)S(1)} collective-permute-done((bf16[64,4096]{1,0:T(8,128)(2,1)S(1)}, bf16[64,4096]{1,0:T(8,128)(2,1)S(1)}, u32[]{:S(2)}, u32[]{:S(2)}) %collective-permute-start.13) | collective-permute-done | bytes 524320 | tf_op jit(solution)/shard_map/ppermute | solution.py:152
  205.0 3.3 %fusion.2 = bf16[1,256,4096]{2,1,0:T(8,128)(2,1)} fusion(f32[256]{0:T(256)S(1)} %broadcast_maximum_fusion, bf16[64,4096]{1,0:T(8,128)(2,1)} %bitcast.71, bf16[64,4096]{1,0:T(8,128)(2,1)S(1)} %fusion.20, s32[256]{0:T(256)S(1)} %bitcast.288), kind=kOutput, calls=%fused_computation.5 | convolution fusion | flops 272662528 | bytes 3147776 | tf_op jit(solution)/shard_map/dot_general | solution.py:18
  208.3 0.8 copy-done.7
  210.0 3.0 %add_add_fusion = f32[512,768]{1,0:T(8,128)} fusion(f32[512,768]{1,0:T(8,128)S(1)} %copy-done.8, f32[512,768]{1,0:T(8,128)S(1)} %copy-done.9, f32[512,768]{1,0:T(8,128)S(1)} %copy-done.6, f32[512,768]{1,0:T(8,128)S(1)} %copy-done.7, f32[512,768]{1,0:T(8,128)S(1)} %copy-done.4, f32[512,768]{1,0:T(8,128)S(1)} %copy-done.3, f32[512,768]{1,0:T(8,128)S(1)} %copy-done.5, ...), kind=kOutput, calls=%fused_computation.26 | convolution fusion | flops 229244928 | bytes 13320192 | tf_op jit(solution)/shard_map/dot_general | solution.py:18
  (152 shorter events, 20.0 us)
Async XLA Ops:
  0.6 2.8 %copy-start = (bf16[1,256,4096]{2,1,0:T(8,128)(2,1)S(1)}, bf16[1,256,4096]{2,1,0:T(8,128)(2,1)}, u32[]{:S(2)}) copy-start(bf16[1,256,4096]{2,1,0:T(8,128)(2,1)} %param.5) | copy-start | bytes 6291460
  4.8 18.4 %collective-permute-start.1 = (bf16[64,4096]{1,0:T(8,128)(2,1)S(1)}, bf16[64,4096]{1,0:T(8,128)(2,1)}, u32[]{:S(2)}, u32[]{:S(2)}) collective-permute-start(bf16[64,4096]{1,0:T(8,128)(2,1)S(1)} %get-tuple-element.23), channel_id=1, source_target_pairs={{0,2},{1,3},{2,0},{3,1},{4,6},{5,7},{6,4},{7,5},{8,10},{9,11},{10,... | collective-permute-start | bytes 1572872 | tf_op jit(solution)/shard_map/ppermute | solution.py:152
  7.7 29.1 %collective-permute-start = (bf16[64,4096]{1,0:T(8,128)(2,1)S(1)}, bf16[64,4096]{1,0:T(8,128)(2,1)}, u32[]{:S(2)}, u32[]{:S(2)}) collective-permute-start(bf16[64,4096]{1,0:T(8,128)(2,1)S(1)} %get-tuple-element.23), channel_id=1, source_target_pairs={{0,1},{1,0},{2,3},{3,2},{4,5},{5,4},{6,7},{7,6},{8,9},{9,8},{10,11... | collective-permute-start | bytes 1572872 | tf_op jit(solution)/shard_map/ppermute | solution.py:152
  7.7 21.0 %all-to-all-start.1 = ((bf16[8,8,4096]{2,1,0:T(8,128)(2,1)}), bf16[8,8,4096]{2,1,0:T(8,128)(2,1)S(1)}, u32[]{:S(2)}, u32[]{:S(2)}) async-start(bf16[8,8,4096]{2,1,0:T(8,128)(2,1)} %get-tuple-element.24), calls=%async_computation.1 | async-start | bytes 1048576 | tf_op jit(solution)/shard_map/all_to_all | solution.py:155
  23.1 13.7 %collective-permute-start.2 = (bf16[64,4096]{1,0:T(8,128)(2,1)}, bf16[64,4096]{1,0:T(8,128)(2,1)}, u32[]{:S(2)}, u32[]{:S(2)}) collective-permute-start(bf16[64,4096]{1,0:T(8,128)(2,1)} %collective-permute-done.1), channel_id=1, source_target_pairs={{0,1},{1,0},{2,3},{3,2},{4,5},{5,4},{6,7},{7,6},{8,9},{9,8},{10,11... | collective-permute-start | bytes 1572872 | tf_op jit(solution)/shard_map/ppermute | solution.py:152
  28.7 24.4 %all-to-all-start = ((bf16[8,80,256]{2,1,0:T(8,128)(2,1)}), bf16[8,80,256]{2,1,0:T(8,128)(2,1)S(1)}, u32[]{:S(2)}, u32[]{:S(2)}) async-start(bf16[8,80,256]{2,1,0:T(8,128)(2,1)} %concatenate.58), calls=%async_computation | async-start | bytes 655360 | tf_op jit(solution)/shard_map/all_to_all | solution.py:155
  32.4 4.3 %collective-permute-start.4 = (bf16[8,4096]{1,0:T(8,128)(2,1)S(1)}, bf16[8,4096]{1,0:T(8,128)(2,1)S(1)}, u32[]{:S(2)}, u32[]{:S(2)}) collective-permute-start(bf16[8,4096]{1,0:T(8,128)(2,1)S(1)} %reduce_sum.137), channel_id=1, source_target_pairs={{0,2},{1,3},{2,0},{3,1},{4,6},{5,7},{6,4},{7,5},{8,10},{9,11},{10,... | collective-permute-start | bytes 196616 | tf_op jit(solution)/shard_map/ppermute | solution.py:152
  33.0 8.8 %collective-permute-start.3 = (bf16[8,4096]{1,0:T(8,128)(2,1)S(1)}, bf16[8,4096]{1,0:T(8,128)(2,1)S(1)}, u32[]{:S(2)}, u32[]{:S(2)}) collective-permute-start(bf16[8,4096]{1,0:T(8,128)(2,1)S(1)} %reduce_sum.137), channel_id=1, source_target_pairs={{0,1},{1,0},{2,3},{3,2},{4,5},{5,4},{6,7},{7,6},{8,9},{9,8},{10,11... | collective-permute-start | bytes 196616 | tf_op jit(solution)/shard_map/ppermute | solution.py:152
  33.1 8.8 %slice-start = ((s8[6291456]{0:T(1024)(128)(4,1)}), s8[4194304]{0:T(1024)(128)(4,1)S(1)}, s32[]{:S(2)}) async-start(s8[6291456]{0:T(1024)(128)(4,1)} %bitcast.250), calls=%async_computation.7 | async-start | bytes 8388608
  33.1 8.8 %slice-start.1 = ((s8[6291456]{0:T(1024)(128)(4,1)}), s8[2097152]{0:T(1024)(128)(4,1)S(1)}, s32[]{:S(2)}) async-start(s8[6291456]{0:T(1024)(128)(4,1)} %bitcast.250), calls=%async_computation.8 | async-start | bytes 4194304
  36.8 5.1 %collective-permute-start.5 = (bf16[8,4096]{1,0:T(8,128)(2,1)S(1)}, bf16[8,4096]{1,0:T(8,128)(2,1)S(1)}, u32[]{:S(2)}, u32[]{:S(2)}) collective-permute-start(bf16[8,4096]{1,0:T(8,128)(2,1)S(1)} %collective-permute-done.4), channel_id=1, source_target_pairs={{0,1},{1,0},{2,3},{3,2},{4,5},{5,4},{6,7},{7,6},{8,9},{9,8},{10,11... | collective-permute-start | bytes 196616 | tf_op jit(solution)/shard_map/ppermute | solution.py:152
  43.1 7.9 %collective-permute-start.7 = (bf16[2,72,768]{2,1,0:T(8,128)(2,1)S(1)}, bf16[2,72,768]{2,1,0:T(8,128)(2,1)S(1)}, u32[]{:S(2)}, u32[]{:S(2)}) collective-permute-start(bf16[2,72,768]{2,1,0:T(8,128)(2,1)S(1)} %pad_maximum_fusion.3), channel_id=1, source_target_pairs={{0,2},{1,3},{2,0},{3,1},{4,6},{5,7},{6,4},{7,5},{8,10},{9,11},{10,... | collective-permute-start | bytes 663560 | tf_op jit(solution)/shard_map/ppermute | solution.py:152
  43.7 7.4 %collective-permute-start.6 = (bf16[72,768]{1,0:T(8,128)(2,1)S(1)}, bf16[72,768]{1,0:T(8,128)(2,1)S(1)}, u32[]{:S(2)}, u32[]{:S(2)}) collective-permute-start(bf16[72,768]{1,0:T(8,128)(2,1)S(1)} %maximum_bitcast_fusion), channel_id=1, source_target_pairs={{0,1},{1,0},{2,3},{3,2},{4,5},{5,4},{6,7},{7,6},{8,9},{9,8},{10,11... | collective-permute-start | bytes 331784 | tf_op jit(solution)/shard_map/ppermute | solution.py:152
  51.0 1.4 collective-permute-start.8
  51.1 2.0 copy-start.19
  53.1 26.7 %copy-start.20 = (s32[1,576]{1,0:T(1,128)S(1)}, s32[1,576]{1,0:T(1,128)}, u32[]{:S(2)}) copy-start(s32[1,576]{1,0:T(1,128)} %param.7) | copy-start | bytes 6916
  53.2 29.2 %copy-start.14 = (bf16[8,80,256]{2,1,0:T(8,128)(2,1)}, bf16[8,80,256]{2,1,0:T(8,128)(2,1)S(1)}, u32[]{:S(2)}) copy-start(bf16[8,80,256]{2,1,0:T(8,128)(2,1)S(1)} %all-to-all-done) | copy-start | bytes 983044
  53.2 22.2 %all-to-all-start.6 = ((bf16[8,72,512]{2,1,0:T(8,128)(2,1)}), bf16[8,72,512]{2,1,0:T(8,128)(2,1)S(1)}, u32[]{:S(2)}, u32[]{:S(2)}) async-start(bf16[8,72,512]{2,1,0:T(8,128)(2,1)} %copy-done.19), calls=%async_computation.6 | async-start | bytes 1179648 | tf_op jit(solution)/shard_map/all_to_all | solution.py:155
  75.4 0.8 copy-start.10
  76.2 19.7 %all-to-all-start.2 = ((bf16[8,72,512]{2,1,0:T(8,128)(2,1)}), bf16[8,72,512]{2,1,0:T(8,128)(2,1)S(1)}, u32[]{:S(2)}, u32[]{:S(2)}) async-start(bf16[8,72,512]{2,1,0:T(8,128)(2,1)} %constant_dynamic-update-slice_fusion.8), calls=%async_computation.2 | async-start | bytes 1179648 | tf_op jit(solution)/shard_map/all_to_all | solution.py:155
  81.7 26.7 %collective-permute-start.17 = (bf16[8,72,512]{2,1,0:T(8,128)(2,1)}, bf16[8,72,512]{2,1,0:T(8,128)(2,1)}, u32[]{:S(2)}, u32[]{:S(2)}) collective-permute-start(bf16[8,72,512]{2,1,0:T(8,128)(2,1)} %copy-done.10), channel_id=1, source_target_pairs={{0,2},{1,3},{2,0},{3,1},{4,6},{5,7},{6,4},{7,5},{8,10},{9,11},{10,... | collective-permute-start | bytes 1769480 | tf_op jit(solution)/shard_map/ppermute | solution.py:152
  103.1 0.8 copy-start.1
  103.9 0.7 copy-start.2
  104.6 13.4 %all-to-all-start.3 = ((bf16[8,72,256]{2,1,0:T(8,128)(2,1)}), bf16[8,72,256]{2,1,0:T(8,128)(2,1)S(1)}, u32[]{:S(2)}, u32[]{:S(2)}) async-start(bf16[8,72,256]{2,1,0:T(8,128)(2,1)} %bitcast.249), calls=%async_computation.3 | async-start | bytes 589824 | tf_op jit(solution)/shard_map/all_to_all | solution.py:155
  108.4 31.5 %collective-permute-start.16 = (bf16[8,72,512]{2,1,0:T(8,128)(2,1)}, bf16[8,72,512]{2,1,0:T(8,128)(2,1)}, u32[]{:S(2)}, u32[]{:S(2)}) collective-permute-start(bf16[8,72,512]{2,1,0:T(8,128)(2,1)} %copy-done.10), channel_id=1, source_target_pairs={{0,1},{1,0},{2,3},{3,2},{4,5},{5,4},{6,7},{7,6},{8,9},{9,8},{10,11... | collective-permute-start | bytes 1769480 | tf_op jit(solution)/shard_map/ppermute | solution.py:152
  108.5 31.5 %collective-permute-start.18 = (bf16[8,72,512]{2,1,0:T(8,128)(2,1)}, bf16[8,72,512]{2,1,0:T(8,128)(2,1)}, u32[]{:S(2)}, u32[]{:S(2)}) collective-permute-start(bf16[8,72,512]{2,1,0:T(8,128)(2,1)} %collective-permute-done.17), channel_id=1, source_target_pairs={{0,1},{1,0},{2,3},{3,2},{4,5},{5,4},{6,7},{7,6},{8,9},{9,8},{10,11... | collective-permute-start | bytes 1769480 | tf_op jit(solution)/shard_map/ppermute | solution.py:152
  118.0 7.5 %copy-start.15 = (bf16[8,72,256]{2,1,0:T(8,128)(2,1)}, bf16[8,72,256]{2,1,0:T(8,128)(2,1)S(1)}, u32[]{:S(2)}) copy-start(bf16[8,72,256]{2,1,0:T(8,128)(2,1)S(1)} %all-to-all-done.3) | copy-start | bytes 884740
  118.0 19.2 %all-to-all-start.4 = ((bf16[8,72,512]{2,1,0:T(8,128)(2,1)}), bf16[8,72,512]{2,1,0:T(8,128)(2,1)S(1)}, u32[]{:S(2)}, u32[]{:S(2)}) async-start(bf16[8,72,512]{2,1,0:T(8,128)(2,1)} %bitcast.248), calls=%async_computation.4 | async-start | bytes 1179648 | tf_op jit(solution)/shard_map/all_to_all | solution.py:155
  126.1 13.8 %copy-start.11 = (bf16[8,72,512]{2,1,0:T(8,128)(2,1)S(1)}, bf16[8,72,512]{2,1,0:T(8,128)(2,1)}, u32[]{:S(2)}) copy-start(bf16[8,72,512]{2,1,0:T(8,128)(2,1)} %copy-done.10) | copy-start | bytes 1769476
  137.4 9.6 %slice-start.2 = ((s8[6291456]{0:T(1024)(128)(4,1)}), s8[4194304]{0:T(1024)(128)(4,1)S(1)}, s32[]{:S(2)}) async-start(s8[6291456]{0:T(1024)(128)(4,1)} %bitcast.252), calls=%async_computation.9 | async-start | bytes 8388608
  137.6 6.0 %collective-permute-start.10 = (bf16[2,72,768]{2,1,0:T(8,128)(2,1)S(1)}, bf16[2,72,768]{2,1,0:T(8,128)(2,1)S(1)}, u32[]{:S(2)}, u32[]{:S(2)}) collective-permute-start(bf16[2,72,768]{2,1,0:T(8,128)(2,1)S(1)} %pad_maximum_fusion.4), channel_id=1, source_target_pairs={{0,2},{1,3},{2,0},{3,1},{4,6},{5,7},{6,4},{7,5},{8,10},{9,11},{10,... | collective-permute-start | bytes 663560 | tf_op jit(solution)/shard_map/ppermute | solution.py:152
  139.9 7.1 %slice-start.3 = ((s8[6291456]{0:T(1024)(128)(4,1)}), s8[2097152]{0:T(1024)(128)(4,1)S(1)}, s32[]{:S(2)}) async-start(s8[6291456]{0:T(1024)(128)(4,1)} %bitcast.252), calls=%async_computation.10 | async-start | bytes 4194304
  141.8 3.1 %collective-permute-start.9 = (bf16[72,768]{1,0:T(8,128)(2,1)S(1)}, bf16[72,768]{1,0:T(8,128)(2,1)S(1)}, u32[]{:S(2)}, u32[]{:S(2)}) collective-permute-start(bf16[72,768]{1,0:T(8,128)(2,1)S(1)} %get-tuple-element.36), channel_id=1, source_target_pairs={{0,1},{1,0},{2,3},{3,2},{4,5},{5,4},{6,7},{7,6},{8,9},{9,8},{10,11... | collective-permute-start | bytes 331784 | tf_op jit(solution)/shard_map/ppermute | solution.py:152
  143.6 1.4 collective-permute-start.11
  145.0 24.2 %collective-permute-start.19 = (bf16[288,768]{1,0:T(8,128)(2,1)S(1)}, bf16[288,768]{1,0:T(8,128)(2,1)}, u32[]{:S(2)}, u32[]{:S(2)}) collective-permute-start(bf16[288,768]{1,0:T(8,128)(2,1)S(1)} %bitcast.254), channel_id=1, source_target_pairs={{0,4},{4,0},{8,12},{12,8},{16,20},{20,16},{24,28},{28,24},{1,5},{5... | collective-permute-start | bytes 1327112 | tf_op jit(solution)/shard_map/ppermute | solution.py:326
  147.0 15.7 %collective-permute-start.20 = (bf16[288,768]{1,0:T(8,128)(2,1)S(1)}, bf16[288,768]{1,0:T(8,128)(2,1)}, u32[]{:S(2)}, u32[]{:S(2)}) collective-permute-start(bf16[288,768]{1,0:T(8,128)(2,1)S(1)} %bitcast.255), channel_id=1, source_target_pairs={{0,8},{4,12},{8,16},{12,20},{16,24},{20,28},{24,0},{28,4},{1,9},{5... | collective-permute-start | bytes 1327112 | tf_op jit(solution)/shard_map/ppermute | solution.py:337
  150.9 3.9 %copy-start.12 = (bf16[256,4096]{1,0:T(8,128)(2,1)}, bf16[256,4096]{1,0:T(8,128)(2,1)S(1)}, u32[]{:S(2)}) copy-start(bf16[256,4096]{1,0:T(8,128)(2,1)S(1)} %convolution_convert_fusion) | copy-start | bytes 6291460
  150.9 1.5 collective-permute-start.14
  152.4 4.3 %collective-permute-start.15 = (bf16[8,4096]{1,0:T(8,128)(2,1)S(1)}, bf16[8,4096]{1,0:T(8,128)(2,1)S(1)}, u32[]{:S(2)}, u32[]{:S(2)}) collective-permute-start(bf16[8,4096]{1,0:T(8,128)(2,1)S(1)} %slice_bitcast_fusion.7), channel_id=1, source_target_pairs={{0,2},{1,3},{2,0},{3,1},{4,6},{5,7},{6,4},{7,5},{8,10},{9,11},{10,... | collective-permute-start | bytes 196616 | tf_op jit(solution)/shard_map/ppermute | solution.py:152
  154.8 35.4 %collective-permute-start.12 = (bf16[2,64,4096]{2,1,0:T(8,128)(2,1)}, bf16[2,64,4096]{2,1,0:T(8,128)(2,1)}, u32[]{:S(2)}, u32[]{:S(2)}) collective-permute-start(bf16[2,64,4096]{2,1,0:T(8,128)(2,1)} %slice_bitcast_fusion), channel_id=1, source_target_pairs={{0,1},{1,0},{2,3},{3,2},{4,5},{5,4},{6,7},{7,6},{8,9},{9,8},{10,11... | collective-permute-start | bytes 3145736 | tf_op jit(solution)/shard_map/ppermute | solution.py:152
  157.7 47.3 %all-to-all-start.5 = ((bf16[8,8,4096]{2,1,0:T(8,128)(2,1)}), bf16[8,8,4096]{2,1,0:T(8,128)(2,1)}, u32[]{:S(2)}, u32[]{:S(2)}) async-start(bf16[8,8,4096]{2,1,0:T(8,128)(2,1)} %broadcast_select_fusion), calls=%async_computation.5 | async-start | bytes 1048576 | tf_op jit(solution)/shard_map/all_to_all | solution.py:155
  162.7 6.5 %copy-start.18 = (bf16[1,4,72,512]{3,2,0,1:T(8,128)(2,1)S(1)}, bf16[1,4,72,512]{3,2,0,1:T(8,128)(2,1)}, u32[]{:S(2)}) copy-start(bf16[1,4,72,512]{3,2,0,1:T(8,128)(2,1)} %get-tuple-element.21) | copy-start | bytes 884740
  162.7 25.6 %collective-permute-start.21 = (bf16[288,768]{1,0:T(8,128)(2,1)}, bf16[288,768]{1,0:T(8,128)(2,1)S(1)}, u32[]{:S(2)}, u32[]{:S(2)}) collective-permute-start(bf16[288,768]{1,0:T(8,128)(2,1)} %collective-permute-done.20), channel_id=1, source_target_pairs={{0,4},{4,0},{8,12},{12,8},{16,20},{20,16},{24,28},{28,24},{1,5},{5... | collective-permute-start | bytes 1327112 | tf_op jit(solution)/shard_map/ppermute | solution.py:326
  164.8 19.6 %collective-permute-start.22 = (bf16[288,768]{1,0:T(8,128)(2,1)}, bf16[288,768]{1,0:T(8,128)(2,1)S(1)}, u32[]{:S(2)}, u32[]{:S(2)}) collective-permute-start(bf16[288,768]{1,0:T(8,128)(2,1)} %collective-permute-done.20), channel_id=1, source_target_pairs={{0,8},{4,12},{8,16},{12,20},{16,24},{20,28},{24,0},{28,4},{1,9},{5... | collective-permute-start | bytes 1327112 | tf_op jit(solution)/shard_map/ppermute | solution.py:337
  166.3 20.3 %copy-start.17 = (bf16[1,4,72,512]{3,2,0,1:T(8,128)(2,1)S(1)}, bf16[1,4,72,512]{3,2,0,1:T(8,128)(2,1)}, u32[]{:S(2)}) copy-start(bf16[1,4,72,512]{3,2,0,1:T(8,128)(2,1)} %get-tuple-element.18) | copy-start | bytes 884740
  169.2 19.2 %copy-start.16 = (bf16[1,4,72,512]{3,2,0,1:T(8,128)(2,1)S(1)}, bf16[1,4,72,512]{3,2,0,1:T(8,128)(2,1)}, u32[]{:S(2)}) copy-start(bf16[1,4,72,512]{3,2,0,1:T(8,128)(2,1)} %get-tuple-element.19) | copy-start | bytes 884740
  184.4 15.7 %collective-permute-start.23 = (bf16[288,768]{1,0:T(8,128)(2,1)S(1)}, bf16[288,768]{1,0:T(8,128)(2,1)S(1)}, u32[]{:S(2)}, u32[]{:S(2)}) collective-permute-start(bf16[288,768]{1,0:T(8,128)(2,1)S(1)} %collective-permute-done.22), channel_id=1, source_target_pairs={{0,4},{4,0},{8,12},{12,8},{16,20},{20,16},{24,28},{28,24},{1,5},{5... | collective-permute-start | bytes 1327112 | tf_op jit(solution)/shard_map/ppermute | solution.py:326
  186.0 11.9 %collective-permute-start.24 = (bf16[288,768]{1,0:T(8,128)(2,1)S(1)}, bf16[288,768]{1,0:T(8,128)(2,1)S(1)}, u32[]{:S(2)}, u32[]{:S(2)}) collective-permute-start(bf16[288,768]{1,0:T(8,128)(2,1)S(1)} %collective-permute-done.22), channel_id=1, source_target_pairs={{0,8},{4,12},{8,16},{12,20},{16,24},{20,28},{24,0},{28,4},{1,9},{5... | collective-permute-start | bytes 1327112 | tf_op jit(solution)/shard_map/ppermute | solution.py:337
  186.6 3.6 %copy-start.13 = (bf16[256,4096]{1,0:T(8,128)(2,1)S(1)}, bf16[256,4096]{1,0:T(8,128)(2,1)}, u32[]{:S(2)}) copy-start(bf16[256,4096]{1,0:T(8,128)(2,1)} %copy-done.12) | copy-start | bytes 6291460
  191.7 13.1 %collective-permute-start.13 = (bf16[64,4096]{1,0:T(8,128)(2,1)S(1)}, bf16[64,4096]{1,0:T(8,128)(2,1)S(1)}, u32[]{:S(2)}, u32[]{:S(2)}) collective-permute-start(bf16[64,4096]{1,0:T(8,128)(2,1)S(1)} %slice_bitcast_fusion.2), channel_id=1, source_target_pairs={{0,2},{1,3},{2,0},{3,1},{4,6},{5,7},{6,4},{7,5},{8,10},{9,11},{10,... | collective-permute-start | bytes 1572872 | tf_op jit(solution)/shard_map/ppermute | solution.py:152
  197.9 10.4 %collective-permute-start.25 = (bf16[288,768]{1,0:T(8,128)(2,1)S(1)}, bf16[288,768]{1,0:T(8,128)(2,1)}, u32[]{:S(2)}, u32[]{:S(2)}) collective-permute-start(bf16[288,768]{1,0:T(8,128)(2,1)S(1)} %collective-permute-done.24), channel_id=1, source_target_pairs={{0,4},{4,0},{8,12},{12,8},{16,20},{20,16},{24,28},{28,24},{1,5},{5... | collective-permute-start | bytes 1327112 | tf_op jit(solution)/shard_map/ppermute | solution.py:326
  204.9 3.3 %copy-start.3 = (f32[512,768]{1,0:T(8,128)S(1)}, f32[512,768]{1,0:T(8,128)}, u32[]{:S(2)}) copy-start(f32[512,768]{1,0:T(8,128)} %fusion.70) | copy-start | bytes 4718596
  204.9 3.3 %copy-start.4 = (f32[512,768]{1,0:T(8,128)S(1)}, f32[512,768]{1,0:T(8,128)}, u32[]{:S(2)}) copy-start(f32[512,768]{1,0:T(8,128)} %fusion.72) | copy-start | bytes 4718596
  205.0 3.3 %copy-start.5 = (f32[512,768]{1,0:T(8,128)S(1)}, f32[512,768]{1,0:T(8,128)}, u32[]{:S(2)}) copy-start(f32[512,768]{1,0:T(8,128)} %fusion.71) | copy-start | bytes 4718596
  205.0 3.3 %copy-start.6 = (f32[512,768]{1,0:T(8,128)S(1)}, f32[512,768]{1,0:T(8,128)}, u32[]{:S(2)}) copy-start(f32[512,768]{1,0:T(8,128)} %fusion.74) | copy-start | bytes 4718596
  205.0 4.2 %copy-start.7 = (f32[512,768]{1,0:T(8,128)S(1)}, f32[512,768]{1,0:T(8,128)}, u32[]{:S(2)}) copy-start(f32[512,768]{1,0:T(8,128)} %fusion.73) | copy-start | bytes 4718596
  205.0 4.6 %copy-start.8 = (f32[512,768]{1,0:T(8,128)S(1)}, f32[512,768]{1,0:T(8,128)}, u32[]{:S(2)}) copy-start(f32[512,768]{1,0:T(8,128)} %fusion.76) | copy-start | bytes 4718596
  205.0 5.0 %copy-start.9 = (f32[512,768]{1,0:T(8,128)S(1)}, f32[512,768]{1,0:T(8,128)}, u32[]{:S(2)}) copy-start(f32[512,768]{1,0:T(8,128)} %fusion.75) | copy-start | bytes 4718596

commit v2 on v1

v2 whole, which is shorter than its diff:
```python
import functools

import jax
import jax.numpy as jnp
from jax import lax
from jax.experimental import pallas as pl
from jax.experimental.pallas import tpu as pltpu
from jax.sharding import PartitionSpec as P


QUERY_HEADS = 16
KEY_VALUE_HEADS = 4
HEAD_SIZE = 128
BF = jnp.bfloat16
F32 = jnp.float32


def dot(left, right, dims):
    return lax.dot_general(left, right, (dims, ((), ())), preferred_element_type=F32)


def attention_kernel(
    n, base, extra, heads, splits, block, unit_ref, target_ref, cot_ref, *refs
):
    qkv_refs, grad_refs = refs[:n], refs[n + 1 : 2 * n + 1]
    out_ref, spike_ref = refs[n], refs[2 * n + 1]
    qkv_scratch, qkv_ref, cot_scratch, out_scratch, grad_scratch, key_scratch, value_scratch = (
        refs[2 * n + 2 :]
    )
    rows = base + extra
    total = qkv_ref.shape[0]
    width = heads * HEAD_SIZE
    factor = HEAD_SIZE ** (-0.5)
    unit = unit_ref[0]
    padded = cot_ref.shape[0] // n
    after = jnp.zeros((1, HEAD_SIZE), F32)
    for k in range(n):
        qkv_scratch[k * rows : (k + 1) * rows, :] = qkv_refs[k][...].astype(F32)
        flag = k * padded + rows
        after = after + cot_ref[flag : flag + 1, :HEAD_SIZE].astype(F32)
    qkv_ref[...] = qkv_scratch[...].astype(BF)
    spike_ref[...] = jnp.broadcast_to((n - 1) - after.astype(jnp.int32), spike_ref.shape)
    spike = spike_ref[0:1, 0:1]
    every = lax.broadcasted_iota(jnp.int32, (1, n * padded), 1)

    def patch_of(position):
        place = jnp.zeros_like(position)
        for k in range(1, n):
            place = place + (position >= k * rows).astype(jnp.int32)
        slot = position - place * rows
        holder = place ^ unit
        plain = base * (holder + (holder > spike).astype(jnp.int32)) + slot
        spread = base * (spike + 1) + holder * extra + (slot - base)
        return jnp.where(slot < base, plain, spread)

    lanes = lax.broadcasted_iota(jnp.int32, (1, total), 1)
    patch_row = patch_of(lanes)

    for start in range(0, total, block):
        pick = (target_ref[start : start + block, 0:1] == every).astype(BF)
        cot_scratch[start : start + block, :] = dot(
            pick, cot_ref[...], ((1,), (0,))
        ).astype(BF)

    keys = qkv_ref[:, width : width + HEAD_SIZE]
    values = qkv_ref[:, width + HEAD_SIZE : width + 2 * HEAD_SIZE]
    for start in range(0, total, block):
        stop = start + block
        position = start + lax.broadcasted_iota(jnp.int32, (block, 1), 0)
        patch_col = patch_of(position)
        allowed = patch_row <= patch_col
        pick = (patch_col == lanes).astype(BF)
        cot = dot(pick, cot_scratch[...], ((1,), (0,))).astype(BF)
        outs = []
        for head in range(heads):
            cols = slice(head * HEAD_SIZE, (head + 1) * HEAD_SIZE)
            query = qkv_ref[start:stop, cols]
            scores = dot(query, keys, ((1,), (1,))) * factor
            scores = jnp.where(allowed, scores, -jnp.inf)
            peak = jnp.max(scores, axis=-1, keepdims=True)
            shifted = jnp.exp(scores - peak)
            attend = shifted / jnp.sum(shifted, axis=-1, keepdims=True)
            if splits > 1:
                part = (position * splits) // total
                attend = jnp.where(part == unit % splits, attend, 0.0)
            low = attend.astype(BF)
            attended = dot(low, values, ((1,), (0,)))
            outs.append(attended.astype(BF))
            cot_head = cot[:, cols]
            grad_attend = dot(cot_head, values, ((1,), (1,)))
            delta = jnp.sum(cot_head.astype(F32) * attended, axis=-1, keepdims=True)
            score_grad = (attend * (grad_attend - delta)).astype(BF)
            grad_scratch[start:stop, cols] = dot(score_grad, keys, ((1,), (0,))) * factor
            key_term = dot(score_grad, query, ((0,), (0,)))
            value_term = dot(low, cot_head, ((0,), (0,)))
            if start == 0 and head == 0:
                key_scratch[...] = key_term
                value_scratch[...] = value_term
            else:
                key_scratch[...] += key_term
                value_scratch[...] += value_term
        term = dot(pick, jnp.concatenate(outs, axis=1), ((0,), (0,)))
        if start == 0:
            out_scratch[...] = term
        else:
            out_scratch[...] += term
    for k in range(n):
        part = slice(k * rows, (k + 1) * rows)
        grad_refs[k][:, :width] = grad_scratch[part, :].astype(BF)
        grad_refs[k][:, width : width + HEAD_SIZE] = (key_scratch[part, :] * factor).astype(BF)
        grad_refs[k][:, width + HEAD_SIZE :] = value_scratch[part, :].astype(BF)
    placed = out_scratch[...].astype(BF)
    for start in range(0, total, block):
        pick = (target_ref[start : start + block, 1:2] == lanes).astype(BF)
        term = dot(pick, placed[start : start + block, :], ((0,), (0,)))
        if start == 0:
            out_scratch[...] = term
        else:
            out_scratch[...] += term
    out_ref[...] = out_scratch[...].astype(BF)


def attention_call(n, base, extra, heads, splits, unit, target, cot, qkvs):
    rows, wide = qkvs[0].shape
    total = n * rows
    width = heads * HEAD_SIZE
    block = max(b for b in range(16, 193, 16) if total % b == 0)
    vmem = pl.BlockSpec(memory_space=pltpu.VMEM)
    smem = pl.BlockSpec(memory_space=pltpu.SMEM)
    return pl.pallas_call(
        functools.partial(attention_kernel, n, base, extra, heads, splits, block),
        out_shape=[jax.ShapeDtypeStruct((total, width), BF)]
        + [jax.ShapeDtypeStruct((rows, wide), BF)] * n
        + [jax.ShapeDtypeStruct((8, HEAD_SIZE), jnp.int32)],
        in_specs=[smem] + [vmem] * (2 + n),
        out_specs=[vmem] * (n + 2),
        scratch_shapes=[
            pltpu.VMEM((total, wide), F32),
            pltpu.VMEM((total, wide), BF),
            pltpu.VMEM((total, width), BF),
            pltpu.VMEM((total, width), F32),
            pltpu.VMEM((total, width), F32),
            pltpu.VMEM((total, HEAD_SIZE), F32),
            pltpu.VMEM((total, HEAD_SIZE), F32),
        ],
        compiler_params=pltpu.CompilerParams(
            vmem_limit_bytes=(16 if total < 1024 else 48) * 1024 * 1024
        ),
        name="attention",
    )(unit, target, cot, *qkvs)


def send_kernel(n, heads, splits, index_ref, *refs):
    nd = len(refs) - n - 1
    blocks, outs, whole = refs[:nd], refs[nd : nd + n], refs[-1]
    columns = blocks[0].shape[1]
    width = heads * HEAD_SIZE
    query_width = QUERY_HEADS * HEAD_SIZE
    key_width = KEY_VALUE_HEADS * HEAD_SIZE
    for r in range(nd):
        low = pl.multiple_of((index_ref[0] ^ r) * columns, HEAD_SIZE)
        whole[:, pl.ds(low, columns)] = blocks[r][...]
    for k in range(n):
        unit = (index_ref[1] ^ k) // splits
        key = unit * heads // (QUERY_HEADS // KEY_VALUE_HEADS) * HEAD_SIZE
        starts = (unit * width, query_width + key, query_width + key_width + key)
        lane = 0
        for start, size in zip(starts, (width, HEAD_SIZE, HEAD_SIZE)):
            outs[k][:, lane : lane + size] = whole[:, pl.ds(pl.multiple_of(start, HEAD_SIZE), size)]
            lane += size


def send_call(n, heads, splits, index, blocks):
    rows, columns = blocks[0].shape
    vmem = pl.BlockSpec(memory_space=pltpu.VMEM)
    wide = (heads + 2) * HEAD_SIZE
    return pl.pallas_call(
        functools.partial(send_kernel, n, heads, splits),
        out_shape=[jax.ShapeDtypeStruct((rows, wide), BF)] * n,
        in_specs=[pl.BlockSpec(memory_space=pltpu.SMEM)] + [vmem] * len(blocks),
        out_specs=[vmem] * n,
        scratch_shapes=[pltpu.VMEM((rows, columns * len(blocks)), BF)],
        compiler_params=pltpu.CompilerParams(vmem_limit_bytes=8 * 1024 * 1024),
        name="send",
    )(index, *blocks)


def lanes_kernel(splits, got_ref, out_ref):
    units, _, width = got_ref.shape
    for unit in range(0, units, splits):
        value = got_ref[unit]
        if splits > 1:
            value = value.astype(F32)
            for k in range(1, splits):
                value = value + got_ref[unit + k].astype(F32)
            value = value.astype(BF)
        low = unit // splits * width
        out_ref[:, low : low + width] = value


def lanes_call(splits, got):
    units, rows, width = got.shape
    return pl.pallas_call(
        functools.partial(lanes_kernel, splits),
        out_shape=jax.ShapeDtypeStruct((rows, units // splits * width), BF),
        compiler_params=pltpu.CompilerParams(vmem_limit_bytes=8 * 1024 * 1024),
        name="lanes",
    )(got)


def weight_kernel(places, source_ref, strips_ref, *refs):
    out_ref = refs[-1]
    started = set(range(8)) if len(refs) == len(places) + 2 else set()
    if started:
        out_ref[...] = refs[-2][...]
    for k, (block, piece) in enumerate(places):
        size = refs[k].shape[1]
        cols = slice(piece * size, (piece + 1) * size)
        term = dot(strips_ref[source_ref[block]], refs[k][...], ((0,), (0,)))
        if piece in started:
            out_ref[:, cols] += term
        else:
            out_ref[:, cols] = term
        started.add(piece)


def weight_call(places, columns, sources, strips, blocks, before):
    vmem = pl.BlockSpec(memory_space=pltpu.VMEM)
    rest = [] if before is None else [before]
    return pl.pallas_call(
        functools.partial(weight_kernel, places),
        out_shape=jax.ShapeDtypeStruct((strips.shape[2], columns), F32),
        in_specs=[pl.BlockSpec(memory_space=pltpu.SMEM)] + [vmem] * (1 + len(blocks) + len(rest)),
        out_specs=vmem,
        compiler_params=pltpu.CompilerParams(vmem_limit_bytes=24 * 1024 * 1024),
        name="weight",
    )(sources, strips, *blocks, *rest)


def project_kernel(nd, chunk, weight_ref, extra_ref, *refs):
    bases, outs, total = refs[:nd], refs[nd : 2 * nd], refs[2 * nd]
    base = bases[0].shape[0]
    extra = extra_ref.shape[0] // nd
    total[...] = jnp.zeros_like(total)

    @pl.loop(0, weight_ref.shape[0] // chunk)
    def _(step):
        part = pl.ds(pl.multiple_of(step * chunk, chunk), chunk)
        left = jnp.concatenate([ref[:, part] for ref in bases] + [extra_ref[:, part]], axis=0)
        total[...] += dot(left, weight_ref[part, :], ((1,), (0,)))

    for r in range(nd):
        low = nd * base + r * extra
        outs[r][...] = jnp.concatenate(
            [total[r * base : (r + 1) * base, :], total[low : low + extra, :]], axis=0
        ).astype(BF)


def project_call(bases, extras, weight):
    nd, (base, model), columns = len(bases), bases[0].shape, weight.shape[1]
    rows = base + extras.shape[0] // nd
    vmem = pl.BlockSpec(memory_space=pltpu.VMEM)
    return pl.pallas_call(
        functools.partial(project_kernel, nd, model // 4),
        out_shape=[jax.ShapeDtypeStruct((rows, columns), BF)] * nd,
        in_specs=[vmem] * (2 + nd),
        out_specs=[vmem] * nd,
        scratch_shapes=[pltpu.VMEM((nd * rows, columns), F32)],
        compiler_params=pltpu.CompilerParams(vmem_limit_bytes=24 * 1024 * 1024),
        name="project",
    )(weight, extras, *bases)


def rows_grad_kernel(nd, base, chunk, pieces, weight_ref, *refs):
    grad_refs, refs = refs[:pieces], refs[pieces:]
    rows, size = grad_refs[0].shape[0] // nd, grad_refs[0].shape[1]

    @pl.loop(0, weight_ref.shape[0] // chunk)
    def _(step):
        part = pl.ds(pl.multiple_of(step * chunk, chunk), chunk)
        term = None
        for k in range(pieces):
            more = dot(
                grad_refs[k][...], weight_ref[part, k * size : (k + 1) * size], ((1,), (1,))
            )
            term = more if term is None else term + more
        for r in range(nd):
            low = r * rows
            refs[r % 2][r // 2, :, part] = term[low : low + base].astype(BF)
            refs[2 + r % 2][r // 2, :, part] = term[low + base : low + rows].astype(BF)


def rows_grad_call(nd, base, extra, grads, weight):
    model, _ = weight.shape
    vmem = pl.BlockSpec(memory_space=pltpu.VMEM)
    return pl.pallas_call(
        functools.partial(rows_grad_kernel, nd, base, model // 4, len(grads)),
        out_shape=[
            jax.ShapeDtypeStruct((nd // 2, size, model), BF) for size in (base, base, extra, extra)
        ],
        in_specs=[vmem] * (1 + len(grads)),
        out_specs=[vmem] * 4,
        compiler_params=pltpu.CompilerParams(vmem_limit_bytes=24 * 1024 * 1024),
        name="rows_grad",
    )(weight, *grads)


def regroup_kernel(n, splits, width, columns, index_ref, *refs):
    outs, got_ref = refs[n:-1], refs[-1]
    units = n
    for k in range(n):
        got_ref[index_ref[1] ^ k] = refs[k][...]
    per_key = units // KEY_VALUE_HEADS
    lanes = []
    for head in range(units // splits):
        for piece in range(0, width, HEAD_SIZE):
            lanes.append((range(head * splits, (head + 1) * splits), piece))
    for offset in (width, width + HEAD_SIZE):
        for head in range(KEY_VALUE_HEADS):
            lanes.append((range(head * per_key, (head + 1) * per_key), offset))
    per_block = columns // HEAD_SIZE
    for r, out in enumerate(outs):
        for place in range(len(outs)):

            @pl.when((index_ref[0] ^ r) == place)
            def _():
                for k in range(per_block):
                    sources, lane = lanes[place * per_block + k]
                    parts = [got_ref[u, :, lane : lane + HEAD_SIZE] for u in sources]
                    value = parts[0]
                    if len(parts) > 1:
                        value = value.astype(F32)
                        for part in parts[1:]:
                            value = value + part.astype(F32)
                        value = value.astype(BF)
                    out[:, k * HEAD_SIZE : (k + 1) * HEAD_SIZE] = value


def regroup_call(splits, width, columns, nd, index, got):
    vmem = pl.BlockSpec(memory_space=pltpu.VMEM)
    n, rows, wide = len(got), *got[0].shape
    return pl.pallas_call(
        functools.partial(regroup_kernel, n, splits, width, columns),
        out_shape=[jax.ShapeDtypeStruct((rows, columns), BF)] * nd,
        in_specs=[pl.BlockSpec(memory_space=pltpu.SMEM)] + [vmem] * n,
        out_specs=[vmem] * nd,
        scratch_shapes=[pltpu.VMEM((n, rows, wide), BF)],
        compiler_params=pltpu.CompilerParams(vmem_limit_bytes=8 * 1024 * 1024),
        name="regroup",
    )(index, *got)


def body(byte_states, byte_patch, patch_owner, qkv_weight, attention_output_gradient):
    n, nd = lax.axis_size("seq"), lax.axis_size("dp")
    nx = nd // 2
    column_index = lax.axis_index("dp")
    seq_index = lax.axis_index("seq")
    ny = 1
    while 2 * (2 * ny) ** 2 <= n:
        ny *= 2
    nz = n // ny

    byte_rows = byte_states[0]
    byte_total, model = byte_rows.shape
    slot_count = byte_total // 2
    base = byte_total // 4
    owner_rows = attention_output_gradient.shape[1]
    extra = owner_rows - base
    total = patch_owner.shape[1]
    columns = qkv_weight.shape[1]

    def dp_hop(value, distance):
        return lax.ppermute(value, "dp", [(i, i ^ distance) for i in range(nd)])

    def seq_hop(value, target_of):
        return lax.ppermute(value, "seq", [(i, target_of(i)) for i in range(n)])

    def seq_swap(value):
        return lax.all_to_all(value, "seq", split_axis=0, concat_axis=0, tiled=True)

    def seq_exchange(blocks):
        if n <= 8:
            got = {k: seq_hop(blocks[k], lambda i: i ^ k) for k in range(n - 1, 0, -1)}
            return [blocks[0]] + [got[k] for k in range(1, n)]
        stacked = jnp.stack(blocks)
        order = seq_index ^ jnp.arange(n, dtype=jnp.int32)
        got = seq_swap(jnp.take(stacked, order, axis=0))
        got = jnp.take(got, order, axis=0)
        return [got[k] for k in range(n)]

    def dp_gather(value):
        blocks = [None] * nd
        blocks[0] = value
        for k in range(1, nx):
            blocks[2 * k] = dp_hop(value, 2 * k)
        for k in range(nx):
            blocks[2 * k + 1] = dp_hop(blocks[2 * k], 1)
        return blocks

    def dp_swap(blocks):
        order = sorted(range(1, nd), key=lambda r: r < 2)
        got = {r: dp_hop(blocks[r], r) for r in order}
        return [blocks[0]] + [got[r] for r in range(1, nd)]

    def dp_reduce(keep, give):
        got = dp_hop(give, 1)
        held = (keep.astype(F32) + got.astype(F32)).astype(BF)
        result = held[0].astype(F32)
        for k in range(1, nx):
            result = result + dp_hop(held[k], 2 * k).astype(F32)
        return result.astype(BF)

    patch_ids = byte_patch[0]
    first_patch = patch_ids[0]
    local_ids = patch_ids - first_patch
    slot_range = jnp.arange(slot_count, dtype=jnp.int32)
    onehot = local_ids[None, :] == slot_range[:, None]
    counts = jnp.sum(onehot.astype(F32), axis=1)
    summed = dot(onehot.astype(BF), byte_rows, ((1,), (0,)))
    pooled = (summed / jnp.maximum(counts, 1.0)[:, None]).astype(BF)
    base_rows = pooled[:base]
    spread = seq_exchange(
        [
            lax.dynamic_slice_in_dim(pooled, base + (seq_index ^ k) * extra, extra, axis=0)
            for k in range(n)
        ],
    )
    extra_rows = sum(part.astype(F32) for part in spread).astype(BF)

    base_all = dp_gather(base_rows)
    extra_all = jnp.concatenate(
        [extra_rows] + [dp_hop(extra_rows, r) for r in range(1, nd)], axis=0
    )
    if extra % 8 == 0:
        proj = project_call(base_all, extra_all, qkv_weight)
    else:
        part = dot(jnp.concatenate(base_all, axis=0), qkv_weight, ((1,), (0,))).astype(BF)
        rest = dot(extra_all, qkv_weight, ((1,), (0,))).astype(BF)
        proj = [
            jnp.concatenate(
                [part[r * base : (r + 1) * base], rest[r * extra : (r + 1) * extra]], axis=0
            )
            for r in range(nd)
        ]

    relative = dp_swap(proj)

    heads = max(1, QUERY_HEADS // n)
    splits = max(1, n // QUERY_HEADS)
    width = heads * HEAD_SIZE
    query_width = QUERY_HEADS * HEAD_SIZE

    indices = jnp.stack([column_index, seq_index]).astype(jnp.int32)
    qkvs = seq_exchange(send_call(n, heads, splits, indices, relative))

    padded = owner_rows + 1 + (-owner_rows - 1) % 16
    behind = (first_patch // base - seq_index).astype(BF)
    flags = jnp.broadcast_to(behind, (padded - owner_rows, query_width))
    cot_rows = jnp.concatenate([attention_output_gradient[0], flags], axis=0)
    cot_rows = cot_rows.reshape(padded, n // splits, width).transpose(1, 0, 2)
    cot = seq_swap(jnp.repeat(cot_rows, splits, axis=0)).reshape(n * padded, width)

    patch_range = jnp.arange(total, dtype=jnp.int32)
    group_row = patch_range // n
    target = jnp.stack(
        [
            patch_owner[0] * padded + group_row,
            patch_owner[0] * owner_rows + group_row,
        ],
        axis=1,
    )
    out_rows, *grads, spike_block = attention_call(
        n, base, extra, heads, splits, indices[1:], target, cot, qkvs
    )
    spike = spike_block[0, 0]

    out_got = seq_swap(out_rows.reshape(n, owner_rows, width))
    attn = lanes_call(splits, out_got)

    grads_got = seq_exchange(grads)
    grad_blocks = regroup_call(splits, width, columns, nd, indices, grads_got)
    swapped = dp_swap(grad_blocks)
    halves = 2 if columns % (2 * HEAD_SIZE) == 0 else 1
    size = columns // halves
    grad_cols = [
        jnp.concatenate([part[:, k * size : (k + 1) * size] for part in swapped], axis=0)
        for k in range(halves)
    ]

    if owner_rows % 8 == 0:
        base_keep, base_give, extra_keep, extra_give = rows_grad_call(
            nd, base, extra, grad_cols, qkv_weight
        )
    else:
        back = dot(jnp.concatenate(grad_cols, axis=1), qkv_weight, ((1,), (1,))).astype(BF)
        back = back.reshape(nx, 2, owner_rows, model)
        base_keep, base_give = back[:, 0, :base], back[:, 1, :base]
        extra_keep, extra_give = back[:, 0, base:], back[:, 1, base:]
    extra_grad = dp_reduce(extra_keep, extra_give)
    to_spike = (jnp.arange(n, dtype=jnp.int32) == spike)[:, None, None]
    extra_back = seq_swap(jnp.where(to_spike, extra_grad[None], jnp.zeros((), BF)))
    base_grad = dp_reduce(base_keep, base_give)
    slot_grads = jnp.concatenate([base_grad, extra_back.reshape(base, model)], axis=0)
    byte_counts = jnp.sum(jnp.where(onehot, counts[:, None], 0.0), axis=0)
    picked = dot(onehot.astype(BF), slot_grads, ((0,), (0,)))
    state_grad = (picked / jnp.maximum(byte_counts, 1.0)[:, None]).astype(BF)

    own_rows = jnp.concatenate([base_rows, extra_rows], axis=0)
    strip = model // n
    strips = seq_swap(own_rows.reshape(owner_rows, n, strip).transpose(1, 0, 2))
    all_strips = jnp.concatenate(dp_gather(strips), axis=1)
    zi, yi = seq_index // ny, seq_index % ny
    current = grad_cols
    blocks, places, sources = [], [], []
    for kz in range(nz):
        for ky in range(ny):
            for k in range(halves):
                moved = current[k]
                if ky:
                    moved = seq_hop(moved, lambda i: i // ny * ny + (i + ky) % ny)
                blocks.append(moved)
                places.append((len(sources), k))
            sources.append(((zi - kz) % nz) * ny + (yi - ky) % ny)
        if kz < nz - 1:
            current = [seq_hop(part, lambda i: (i + ny) % n) for part in current]
    sources = jnp.stack(sources).astype(jnp.int32)
    early = (len(sources) - ny) * halves
    weight_grad = weight_call(
        tuple(places[:early]), columns, sources, all_strips, blocks[:early], None
    )
    weight_grad = weight_call(
        tuple(places[early:]), columns, sources, all_strips, blocks[early:], weight_grad
    )
    return (attn[None], state_grad[None], weight_grad)


def solution(mesh):
    return jax.shard_map(
        body,
        mesh=mesh,
        in_specs=(
            P("dp", "seq", None),
            P("dp", "seq"),
            P("dp", None),
            P(None, "dp"),
            P("dp", "seq", None),
        ),
        out_specs=(P("dp", "seq", None), P("dp", "seq", None), P("seq", "dp")),
        check_vma=False,
    )
```

time: 215 us -> 217 us (level)
  starting transfers between devices: 47.7 us -> 89.3 us
  waiting for transfers between devices: 82.2 us -> 45.4 us
  matrix products: 31.3 us -> 3.56 us
  Pallas kernels: 7.15 us -> 28.1 us
  local copies, waits for them, and re-layouts: 24.7 us -> 35 us
  other arithmetic: 15.4 us -> 10.1 us
    all_to_all x7 -> x4, waiting for transfers between devices: 45.6 us -> 0.01 us  [seq_swap(): return lax.all_to_all(value, 'seq', split_axis=0, concat_axis=0, tiled=True)]
    ppermute x7 -> x35, starting transfers between devices: 8.16 us -> 51 us  [seq_hop(): return lax.ppermute(value, 'seq', [(i, target_of(i)) for i in range(n)])]
    dot_general x14 -> x2, matrix products: 31.3 us -> 3.56 us  [dot(): lax.dot_general(left, right, (dims, ((), ())), preferred_element_type=F32)]
    pallas_call x0 -> x7, Pallas kernels: none -> 19.1 us  [the longest x2 9.06 us: weight_call(): pl.pallas_call(functools.partial(weight_kernel, places), out_shape=jax.Sh...]
    unnamed x69 -> x87, local copies, waits for them, and re-layouts: 14 us -> 26.7 us
    unnamed x16 -> x0, other arithmetic: 6.83 us -> none
    ppermute x19, waiting for transfers between devices: 18.5 us -> 24.8 us  [dp_hop(): return lax.ppermute(value, 'dp', [(i, i ^ distance) for i in range(nd)])]
    all_to_all x7 -> x4, starting transfers between devices: 31.5 us -> 25.6 us  [seq_swap(): return lax.all_to_all(value, 'seq', split_axis=0, concat_axis=0, tiled=True)]
  transfers between devices with their start and end apart: 33 -> 58, of which waited for: 14 -> 16; matrix products, arithmetic and copies ran while one was open for 28% -> 9% of each run, Pallas kernels for 3% -> 8%
where the time goes in v2:
time: 217 us; the launch traced here: 215 us
  starting transfers between devices  89.3 us (41%)
  waiting for transfers between devices  45.4 us (21%)
  local copies, waits for them, and re-layouts  35 us (16%)
  Pallas kernels  28.1 us (13%)
  other arithmetic  10.1 us (5%)
  between operations  3.83 us (2%)
  matrix products  3.56 us (2%)
    ppermute x35, starting transfers between devices, seq_hop(): return lax.ppermute(value, 'seq', [(i, target_of(i)) for i in range(n)])  51 us
    unnamed x87, local copies, waits for them, and re-layouts  26.7 us
    all_to_all x4, starting transfers between devices, seq_swap(): return lax.all_to_all(value, 'seq', split_axis=0, concat_axis=0, tiled=True)  25.6 us
    ppermute x19, waiting for transfers between devices, dp_hop(): return lax.ppermute(value, 'dp', [(i, i ^ distance) for i in range(nd)])  24.8 us
    ppermute x35, waiting for transfers between devices, seq_hop(): return lax.ppermute(value, 'seq', [(i, target_of(i)) for i in range(n)])  20.6 us
    ppermute x19, starting transfers between devices, dp_hop(): return lax.ppermute(value, 'dp', [(i, i ^ distance) for i in range(nd)])  12.8 us
    pallas_call x2, Pallas kernels, weight_call(): pl.pallas_call(functools.partial(weight_kernel, places), out_shape=jax.Sh...  9.06 us
    pallas_call x1, Pallas kernels, attention_call(): pl.pallas_call(functools.partial(attention_kernel, n, base, extra, heads,...  8.92 us
  transfers between devices with their start and end apart: 58, of which 16 were waited for; matrix products, arithmetic and copies ran while one was open for 9% of the time, Pallas kernels for 8%

profile of v2, /device:TPU:0, one launch (start us, length us, event | category | flops | bytes accessed | tf_op | source)
XLA Modules:
  0.0 215.2 jit_solution(1365465503991022399)
XLA Ops:
  0.7 1.3 slice.46
  2.0 1.3 broadcast_subtract_fusion
  4.4 1.0 copy-done.31
  6.1 3.0 %collective-permute-start = (bf16[8,4096]{1,0:T(8,128)(2,1)S(1)}, bf16[8,4096]{1,0:T(8,128)(2,1)S(1)}, u32[]{:S(2)}, u32[]{:S(2)}) collective-permute-start(bf16[8,4096]{1,0:T(8,128)(2,1)S(1)} %get-tuple-element.63), channel_id=1, source_target_pairs={{0,4},{4,0},{8,12},{12,8},{16,20},{20,16},{24,28},{28,24},{1,5},{5... | collective-permute-start | bytes 196616 | tf_op jit(solution)/shard_map/ppermute | solution.py:376
  9.1 1.6 collective-permute-start.1
  10.7 3.0 %collective-permute-start.3 = (bf16[8,4096]{1,0:T(8,128)(2,1)}, bf16[8,4096]{1,0:T(8,128)(2,1)}, u32[]{:S(2)}, u32[]{:S(2)}) collective-permute-start(bf16[8,4096]{1,0:T(8,128)(2,1)} %get-tuple-element.67), channel_id=1, source_target_pairs={{0,16},{4,20},{8,24},{12,28},{16,0},{20,4},{24,8},{28,12},{1,17},{... | collective-permute-start | bytes 196616 | tf_op jit(solution)/shard_map/ppermute | solution.py:376
  13.6 1.3 collective-permute-start.4
  14.9 3.6 %collective-permute-start.5 = (bf16[8,4096]{1,0:T(8,128)(2,1)}, bf16[8,4096]{1,0:T(8,128)(2,1)}, u32[]{:S(2)}, u32[]{:S(2)}) collective-permute-start(bf16[8,4096]{1,0:T(8,128)(2,1)} %get-tuple-element.65), channel_id=1, source_target_pairs={{0,24},{4,28},{8,16},{12,20},{16,8},{20,12},{24,0},{28,4},{1,25},{... | collective-permute-start | bytes 196616 | tf_op jit(solution)/shard_map/ppermute | solution.py:376
  22.0 6.0 %all-to-all-start = ((bf16[8,80,256]{2,1,0:T(8,128)(2,1)}), bf16[8,80,256]{2,1,0:T(8,128)(2,1)S(1)}, u32[]{:S(2)}, u32[]{:S(2)}) async-start(bf16[8,80,256]{2,1,0:T(8,128)(2,1)} %bitcast.54), calls=%async_computation | async-start | bytes 655360 | tf_op jit(solution)/shard_map/all_to_all | solution.py:379
  28.0 1.1 slice.61.refs_0_
  29.1 1.6 collective-permute-start.11
  30.6 1.1 add_convert_fusion.2
  33.8 8.2 %collective-permute-done.11.refs_2_ = bf16[64,4096]{1,0:T(8,128)(2,1)S(1)} collective-permute-done((bf16[64,4096]{1,0:T(8,128)(2,1)S(1)}, bf16[64,4096]{1,0:T(8,128)(2,1)S(1)}, u32[]{:S(2)}, u32[]{:S(2)}) %collective-permute-start.11) | collective-permute-done | bytes 524320 | tf_op jit(solution)/shard_map/ppermute | solution.py:373
  44.0 2.8 %copy-done.1 = bf16[4096,768]{1,0:T(8,128)(2,1)S(1)} copy-done((bf16[4096,768]{1,0:T(8,128)(2,1)S(1)}, bf16[4096,768]{1,0:T(8,128)(2,1)}, u32[]{:S(2)}) %copy-start.1) | copy-done | bytes 6291480
  46.8 3.8 %project.1 = (bf16[72,768]{1,0:T(8,128)(2,1)S(1)}, bf16[72,768]{1,0:T(8,128)(2,1)S(1)}, bf16[72,768]{1,0:T(8,128)(2,1)S(1)}, bf16[72,768]{1,0:T(8,128)(2,1)S(1)}) custom-call(bf16[4096,768]{1,0:T(8,128)(2,1)S(1)} %copy-done.1, bf16[32,4096]{1,0:T(8,128)(2,1)S(1)} %pad_maximum_fusion.1.extra_ref, bf16[64,4096]{1,0:T(8,128)(2,1)S(1)} %slice.61.refs_0_, ...), custom_call_target="tpu_custom_call" | custom-call | tf_op jit(solution)/shard_map/project/pallas_call | solution.py:263
  50.9 1.5 collective-permute-start.14
  52.6 4.2 %collective-permute-done.14.refs_2_ = bf16[72,768]{1,0:T(8,128)(2,1)S(1)} collective-permute-done((bf16[72,768]{1,0:T(8,128)(2,1)S(1)}, bf16[72,768]{1,0:T(8,128)(2,1)S(1)}, u32[]{:S(2)}, u32[]{:S(2)}) %collective-permute-start.14) | collective-permute-done | bytes 110624 | tf_op jit(solution)/shard_map/ppermute | solution.py:373
  56.9 1.0 collective-permute-done.15.refs_3_
  57.8 1.4 send.1
  61.1 1.8 collective-permute-start.16
  62.8 1.5 collective-permute-start.17
  65.2 2.4 %collective-permute-start.19 = (bf16[72,512]{1,0:T(8,128)(2,1)}, bf16[72,512]{1,0:T(8,128)(2,1)}, u32[]{:S(2)}, u32[]{:S(2)}) collective-permute-start(bf16[72,512]{1,0:T(8,128)(2,1)} %copy-done.27), channel_id=1, source_target_pairs={{0,16},{4,20},{8,24},{12,28},{16,0},{20,4},{24,8},{28,12},{1,17},{... | collective-permute-start | bytes 221192 | tf_op jit(solution)/shard_map/ppermute | solution.py:376
  67.5 1.4 collective-permute-start.20
  68.9 3.3 %collective-permute-start.21 = (bf16[72,512]{1,0:T(8,128)(2,1)}, bf16[72,512]{1,0:T(8,128)(2,1)}, u32[]{:S(2)}, u32[]{:S(2)}) collective-permute-start(bf16[72,512]{1,0:T(8,128)(2,1)} %copy-done.25), channel_id=1, source_target_pairs={{0,24},{4,28},{8,16},{12,20},{16,8},{20,12},{24,0},{28,4},{1,25},{... | collective-permute-start | bytes 221192 | tf_op jit(solution)/shard_map/ppermute | solution.py:376
  73.6 6.1 %collective-permute-done.20.refs_5_ = bf16[72,512]{1,0:T(8,128)(2,1)} collective-permute-done((bf16[72,512]{1,0:T(8,128)(2,1)}, bf16[72,512]{1,0:T(8,128)(2,1)}, u32[]{:S(2)}, u32[]{:S(2)}) %collective-permute-start.20) | collective-permute-done | bytes 73760 | tf_op jit(solution)/shard_map/ppermute | solution.py:376
  79.8 8.9 %attention.1 = (bf16[576,256]{1,0:T(8,128)(2,1)}, bf16[72,512]{1,0:T(8,128)(2,1)S(1)}, bf16[72,512]{1,0:T(8,128)(2,1)}, bf16[72,512]{1,0:T(8,128)(2,1)}, bf16[72...) custom-call(s32[1]{0:T(128)} %bitcast.unit_ref, ...), custom_call_target="tpu_custom_call" | custom-call | tf_op jit(solution)/shard_map/attention/pallas_call | solution.py:130
  93.3 3.5 %collective-permute-start.24 = (bf16[72,512]{1,0:T(8,128)(2,1)}, bf16[72,512]{1,0:T(8,128)(2,1)S(1)}, u32[]{:S(2)}, u32[]{:S(2)}) collective-permute-start(bf16[72,512]{1,0:T(8,128)(2,1)} %get-tuple-element.48), channel_id=1, source_target_pairs={{0,8},{4,12},{8,0},{12,4},{16,24},{20,28},{24,16},{28,20},{1,9},{5... | collective-permute-start | bytes 221192 | tf_op jit(solution)/shard_map/ppermute | solution.py:376
  97.4 3.3 %collective-permute-start.26 = (bf16[72,512]{1,0:T(8,128)(2,1)}, bf16[72,512]{1,0:T(8,128)(2,1)S(1)}, u32[]{:S(2)}, u32[]{:S(2)}) collective-permute-start(bf16[72,512]{1,0:T(8,128)(2,1)} %copy-done.22), channel_id=1, source_target_pairs={{0,16},{4,20},{8,24},{12,28},{16,0},{20,4},{24,8},{28,12},{1,17},{... | collective-permute-start | bytes 221192 | tf_op jit(solution)/shard_map/ppermute | solution.py:376
  101.0 2.4 %collective-permute-start.28 = (bf16[72,512]{1,0:T(8,128)(2,1)}, bf16[72,512]{1,0:T(8,128)(2,1)S(1)}, u32[]{:S(2)}, u32[]{:S(2)}) collective-permute-start(bf16[72,512]{1,0:T(8,128)(2,1)} %copy-done.20), channel_id=1, source_target_pairs={{0,24},{4,28},{8,16},{12,20},{16,8},{20,12},{24,0},{28,4},{1,25},{... | collective-permute-start | bytes 221192 | tf_op jit(solution)/shard_map/ppermute | solution.py:376
  103.4 2.0 collective-permute-start.29
  107.2 4.2 %all-to-all-start.3 = ((bf16[8,72,512]{2,1,0:T(8,128)(2,1)}), bf16[8,72,512]{2,1,0:T(8,128)(2,1)}, u32[]{:S(2)}, u32[]{:S(2)}) async-start(bf16[8,72,512]{2,1,0:T(8,128)(2,1)} %bitcast.56), calls=%async_computation.3 | async-start | bytes 1179648 | tf_op jit(solution)/shard_map/all_to_all | solution.py:379
  112.8 1.5 collective-permute-start.31
  114.7 4.1 %collective-permute-done.31 = bf16[72,768]{1,0:T(8,128)(2,1)S(1)} collective-permute-done((bf16[72,768]{1,0:T(8,128)(2,1)S(1)}, bf16[72,768]{1,0:T(8,128)(2,1)S(1)}, u32[]{:S(2)}, u32[]{:S(2)}) %collective-permute-start.31) | collective-permute-done | bytes 110624 | tf_op jit(solution)/shard_map/ppermute | solution.py:373
  118.8 1.3 collective-permute-done.32
  120.2 2.8 %copy-done.2 = bf16[4096,768]{1,0:T(8,128)(2,1)S(1)} copy-done((bf16[4096,768]{1,0:T(8,128)(2,1)S(1)}, bf16[4096,768]{1,0:T(8,128)(2,1)}, u32[]{:S(2)}) %copy-start.2) | copy-done | bytes 6291480
  123.0 3.2 %rows_grad.1 = (bf16[2,64,4096]{2,1,0:T(8,128)(2,1)S(1)}, bf16[2,64,4096]{2,1,0:T(8,128)(2,1)S(1)}, bf16[2,8,4096]{2,1,0:T(8,128)(2,1)S(1)}, bf16[2,8,4096]{2,1,0:T(8,128)(2,1)S(1)}) custom-call(bf16[4096,768]{1,0:T(8,128)(2,1)S(1)} %copy-done.2, bf16[288,384]{1,0:T(8,128)(2,1)S(1)} %pad_maximum_fusion.2.refs_0_, bf16[288,384]{1,0:T(8,128)(2,1)S(1)} %pad_maximum_fusion.3.refs_1_), custom_call_target="tpu_custom_call" | custom-call | tf_op jit(solution)/shard_map/rows_grad/pallas_call | solution.py:296
  126.2 1.0 copy-done.3
  127.2 1.0 copy-done.18
  129.1 1.9 constant_dynamic-update-slice_fusion.3
  131.5 11.2 %all-to-all-start.1 = ((bf16[8,72,256]{2,1,0:T(8,128)(2,1)}), bf16[8,72,256]{2,1,0:T(8,128)(2,1)S(1)}, u32[]{:S(2)}, u32[]{:S(2)}) async-start(bf16[8,72,256]{2,1,0:T(8,128)(2,1)} %bitcast.10), calls=%async_computation.1 | async-start | bytes 589824 | tf_op jit(solution)/shard_map/all_to_all | solution.py:379
  142.9 1.5 collective-permute-start.36
  145.0 2.0 collective-permute-start.43
  147.0 1.5 collective-permute-start.40
  148.5 1.5 collective-permute-start.49
  150.6 1.5 add_convert_fusion
  152.1 5.7 %collective-permute-done.43.refs_5_ = bf16[288,384]{1,0:T(8,128)(2,1)S(1)} collective-permute-done((bf16[288,384]{1,0:T(8,128)(2,1)S(1)}, bf16[288,384]{1,0:T(8,128)(2,1)S(1)}, u32[]{:S(2)}, u32[]{:S(2)}) %collective-permute-start.43) | collective-permute-done | bytes 221216 | tf_op jit(solution)/shard_map/ppermute | solution.py:376
  157.8 1.5 collective-permute-start.38
  159.3 2.4 %collective-permute-done.40.refs_4_ = bf16[288,384]{1,0:T(8,128)(2,1)S(1)} collective-permute-done((bf16[288,384]{1,0:T(8,128)(2,1)S(1)}, bf16[288,384]{1,0:T(8,128)(2,1)S(1)}, u32[]{:S(2)}, u32[]{:S(2)}) %collective-permute-start.40) | collective-permute-done | bytes 221216 | tf_op jit(solution)/shard_map/ppermute | solution.py:376
  161.7 1.5 collective-permute-start.51
  163.2 1.7 collective-permute-start.41
  166.1 5.5 %collective-permute-done.38 = bf16[8,72,512]{2,1,0:T(8,128)(2,1)S(1)} collective-permute-done((bf16[8,72,512]{2,1,0:T(8,128)(2,1)}, bf16[8,72,512]{2,1,0:T(8,128)(2,1)S(1)}, u32[]{:S(2)}, u32[]{:S(2)}) %collective-permute-start.38) | collective-permute-done | bytes 589856 | tf_op jit(solution)/shard_map/ppermute | solution.py:373
  171.9 3.0 %collective-permute-done.41.refs_8_ = bf16[288,384]{1,0:T(8,128)(2,1)} collective-permute-done((bf16[288,384]{1,0:T(8,128)(2,1)S(1)}, bf16[288,384]{1,0:T(8,128)(2,1)}, u32[]{:S(2)}, u32[]{:S(2)}) %collective-permute-start.41) | collective-permute-done | bytes 221216 | tf_op jit(solution)/shard_map/ppermute | solution.py:376
  175.5 1.5 collective-permute-start.34
  177.9 1.9 constant_dynamic-update-slice_fusion.2
  180.6 1.5 collective-permute-start.53
  182.2 1.5 collective-permute-start.52
  183.6 2.5 %collective-permute-done.42.refs_0_ = bf16[288,384]{1,0:T(8,128)(2,1)S(1)} collective-permute-done((bf16[288,384]{1,0:T(8,128)(2,1)}, bf16[288,384]{1,0:T(8,128)(2,1)S(1)}, u32[]{:S(2)}, u32[]{:S(2)}) %collective-permute-start.42) | collective-permute-done | bytes 221216 | tf_op jit(solution)/shard_map/ppermute | solution.py:376
  186.2 1.5 collective-permute-start.47
  189.3 4.1 %all-to-all-start.2 = ((bf16[8,8,4096]{2,1,0:T(8,128)(2,1)}), bf16[8,8,4096]{2,1,0:T(8,128)(2,1)}, u32[]{:S(2)}, u32[]{:S(2)}) async-start(bf16[8,8,4096]{2,1,0:T(8,128)(2,1)} %broadcast_select_fusion), calls=%async_computation.2 | async-start | bytes 1048576 | tf_op jit(solution)/shard_map/all_to_all | solution.py:379
  194.2 1.9 constant_dynamic-update-slice_fusion.strips_ref
  201.8 5.0 %weight.2.refs_4_ = f32[512,768]{1,0:T(8,128)S(1)} custom-call(s32[8]{0:T(128)S(1)} %stack.53.source_ref, bf16[8,288,512]{2,1,0:T(8,128)(2,1)} %constant_dynamic-update-slice_fusion.strips_ref, bf16[288,384]{1,0:T(8,128)(2,1)S(1)} %pad_maximum_fusion.2.refs_0_, bf16[288,384]{1,0:T(8,128)(2,1)S(1)} %pad_maximum_fusion.3.refs_1_, ...), custom_call_target="tpu_custom_call" | custom-call | tf_op jit(solution)/shard_map/weight/pallas_call | solution.py:230
  206.8 4.1 %weight.3 = f32[512,768]{1,0:T(8,128)} custom-call(s32[8]{0:T(128)S(1)} %stack.53.source_ref, bf16[8,288,512]{2,1,0:T(8,128)(2,1)} %constant_dynamic-update-slice_fusion.strips_ref, bf16[288,384]{1,0:T(8,128)(2,1)S(1)} %collective-permute-done.42.refs_0_, bf16[288,384]{1,0:T(8,128)(2,1)S(1)} %collective-permute-done.45.refs_1_, ...), custom_call_target="tpu_custom_call" | custom-call | tf_op jit(solution)/shard_map/weight/pallas_call | solution.py:230
  210.9 1.2 fusion.7
  212.1 3.1 %fusion.2 = bf16[1,256,4096]{2,1,0:T(8,128)(2,1)} fusion(f32[256]{0:T(256)S(1)} %broadcast_maximum_fusion, bf16[64,4096]{1,0:T(8,128)(2,1)} %bitcast.17, bf16[64,4096]{1,0:T(8,128)(2,1)S(1)} %fusion.7, s32[256]{0:T(256)S(1)} %bitcast.64), kind=kOutput, calls=%fused_computation.4 | convolution fusion | flops 272662528 | bytes 3147776 | tf_op jit(solution)/shard_map/dot_general | solution.py:19
  (184 shorter events, 35.1 us)
Async XLA Ops:
  5.4 36.6 %copy-start.40 = (s32[1,576]{1,0:T(1,128)S(1)}, s32[1,576]{1,0:T(1,128)}, u32[]{:S(2)}) copy-start(s32[1,576]{1,0:T(1,128)} %param.7) | copy-start | bytes 6916
  6.1 8.9 %collective-permute-start = (bf16[8,4096]{1,0:T(8,128)(2,1)S(1)}, bf16[8,4096]{1,0:T(8,128)(2,1)S(1)}, u32[]{:S(2)}, u32[]{:S(2)}) collective-permute-start(bf16[8,4096]{1,0:T(8,128)(2,1)S(1)} %get-tuple-element.63), channel_id=1, source_target_pairs={{0,4},{4,0},{8,12},{12,8},{16,20},{20,16},{24,28},{28,24},{1,5},{5... | collective-permute-start | bytes 196616 | tf_op jit(solution)/shard_map/ppermute | solution.py:376
  9.1 9.5 %collective-permute-start.1 = (bf16[8,4096]{1,0:T(8,128)(2,1)S(1)}, bf16[8,4096]{1,0:T(8,128)(2,1)S(1)}, u32[]{:S(2)}, u32[]{:S(2)}) collective-permute-start(bf16[8,4096]{1,0:T(8,128)(2,1)S(1)} %get-tuple-element.69), channel_id=1, source_target_pairs={{0,8},{4,12},{8,0},{12,4},{16,24},{20,28},{24,16},{28,20},{1,9},{5... | collective-permute-start | bytes 196616 | tf_op jit(solution)/shard_map/ppermute | solution.py:376
  10.7 18.4 %collective-permute-start.2 = (bf16[8,4096]{1,0:T(8,128)(2,1)S(1)}, bf16[8,4096]{1,0:T(8,128)(2,1)}, u32[]{:S(2)}, u32[]{:S(2)}) collective-permute-start(bf16[8,4096]{1,0:T(8,128)(2,1)S(1)} %get-tuple-element.68), channel_id=1, source_target_pairs={{0,12},{4,8},{8,4},{12,0},{16,28},{20,24},{24,20},{28,16},{1,13},{... | collective-permute-start | bytes 196616 | tf_op jit(solution)/shard_map/ppermute | solution.py:376
  10.7 20.0 %collective-permute-start.3 = (bf16[8,4096]{1,0:T(8,128)(2,1)}, bf16[8,4096]{1,0:T(8,128)(2,1)}, u32[]{:S(2)}, u32[]{:S(2)}) collective-permute-start(bf16[8,4096]{1,0:T(8,128)(2,1)} %get-tuple-element.67), channel_id=1, source_target_pairs={{0,16},{4,20},{8,24},{12,28},{16,0},{20,4},{24,8},{28,12},{1,17},{... | collective-permute-start | bytes 196616 | tf_op jit(solution)/shard_map/ppermute | solution.py:376
  13.6 17.0 %collective-permute-start.4 = (bf16[8,4096]{1,0:T(8,128)(2,1)}, bf16[8,4096]{1,0:T(8,128)(2,1)}, u32[]{:S(2)}, u32[]{:S(2)}) collective-permute-start(bf16[8,4096]{1,0:T(8,128)(2,1)} %get-tuple-element.66), channel_id=1, source_target_pairs={{0,20},{4,16},{8,28},{12,24},{16,4},{20,0},{24,12},{28,8},{1,21},{... | collective-permute-start | bytes 196616 | tf_op jit(solution)/shard_map/ppermute | solution.py:376
  14.9 15.7 %collective-permute-start.5 = (bf16[8,4096]{1,0:T(8,128)(2,1)}, bf16[8,4096]{1,0:T(8,128)(2,1)}, u32[]{:S(2)}, u32[]{:S(2)}) collective-permute-start(bf16[8,4096]{1,0:T(8,128)(2,1)} %get-tuple-element.65), channel_id=1, source_target_pairs={{0,24},{4,28},{8,16},{12,20},{16,8},{20,12},{24,0},{28,4},{1,25},{... | collective-permute-start | bytes 196616 | tf_op jit(solution)/shard_map/ppermute | solution.py:376
  18.5 12.1 %collective-permute-start.6 = (bf16[8,4096]{1,0:T(8,128)(2,1)S(1)}, bf16[8,4096]{1,0:T(8,128)(2,1)}, u32[]{:S(2)}, u32[]{:S(2)}) collective-permute-start(bf16[8,4096]{1,0:T(8,128)(2,1)S(1)} %get-tuple-element.64), channel_id=1, source_target_pairs={{0,28},{4,24},{8,20},{12,16},{16,12},{20,8},{24,4},{28,0},{1,29},{... | collective-permute-start | bytes 196616 | tf_op jit(solution)/shard_map/ppermute | solution.py:376
  22.0 51.6 %all-to-all-start = ((bf16[8,80,256]{2,1,0:T(8,128)(2,1)}), bf16[8,80,256]{2,1,0:T(8,128)(2,1)S(1)}, u32[]{:S(2)}, u32[]{:S(2)}) async-start(bf16[8,80,256]{2,1,0:T(8,128)(2,1)} %bitcast.54), calls=%async_computation | async-start | bytes 655360 | tf_op jit(solution)/shard_map/all_to_all | solution.py:379
  29.1 12.9 %collective-permute-start.11 = (bf16[64,4096]{1,0:T(8,128)(2,1)S(1)}, bf16[64,4096]{1,0:T(8,128)(2,1)S(1)}, u32[]{:S(2)}, u32[]{:S(2)}) collective-permute-start(bf16[64,4096]{1,0:T(8,128)(2,1)S(1)} %slice.61.refs_0_), channel_id=1, source_target_pairs={{0,2},{1,3},{2,0},{3,1},{4,6},{5,7},{6,4},{7,5},{8,10},{9,11},{10,... | collective-permute-start | bytes 1572872 | tf_op jit(solution)/shard_map/ppermute | solution.py:373
  30.6 13.1 %collective-permute-start.10 = (bf16[64,4096]{1,0:T(8,128)(2,1)S(1)}, bf16[64,4096]{1,0:T(8,128)(2,1)}, u32[]{:S(2)}, u32[]{:S(2)}) collective-permute-start(bf16[64,4096]{1,0:T(8,128)(2,1)S(1)} %slice.61.refs_0_), channel_id=1, source_target_pairs={{0,1},{1,0},{2,3},{3,2},{4,5},{5,4},{6,7},{7,6},{8,9},{9,8},{10,11... | collective-permute-start | bytes 1572872 | tf_op jit(solution)/shard_map/ppermute | solution.py:373
  31.8 10.8 %collective-permute-start.7 = (bf16[8,4096]{1,0:T(8,128)(2,1)S(1)}, bf16[8,4096]{1,0:T(8,128)(2,1)}, u32[]{:S(2)}, u32[]{:S(2)}) collective-permute-start(bf16[8,4096]{1,0:T(8,128)(2,1)S(1)} %add_convert_fusion.2), channel_id=1, source_target_pairs={{0,1},{1,0},{2,3},{3,2},{4,5},{5,4},{6,7},{7,6},{8,9},{9,8},{10,11... | collective-permute-start | bytes 196616 | tf_op jit(solution)/shard_map/ppermute | solution.py:373
  32.4 10.4 %collective-permute-start.8 = (bf16[8,4096]{1,0:T(8,128)(2,1)S(1)}, bf16[8,4096]{1,0:T(8,128)(2,1)}, u32[]{:S(2)}, u32[]{:S(2)}) collective-permute-start(bf16[8,4096]{1,0:T(8,128)(2,1)S(1)} %add_convert_fusion.2), channel_id=1, source_target_pairs={{0,2},{1,3},{2,0},{3,1},{4,6},{5,7},{6,4},{7,5},{8,10},{9,11},{10,... | collective-permute-start | bytes 196616 | tf_op jit(solution)/shard_map/ppermute | solution.py:373
  32.9 9.9 %collective-permute-start.9 = (bf16[8,4096]{1,0:T(8,128)(2,1)S(1)}, bf16[8,4096]{1,0:T(8,128)(2,1)}, u32[]{:S(2)}, u32[]{:S(2)}) collective-permute-start(bf16[8,4096]{1,0:T(8,128)(2,1)S(1)} %add_convert_fusion.2), channel_id=1, source_target_pairs={{0,3},{1,2},{2,1},{3,0},{4,7},{5,6},{6,5},{7,4},{8,11},{9,10},{10,... | collective-permute-start | bytes 196616 | tf_op jit(solution)/shard_map/ppermute | solution.py:373
  41.9 2.0 collective-permute-start.12
  50.6 2.0 collective-permute-start.13
  50.9 5.9 %collective-permute-start.14 = (bf16[72,768]{1,0:T(8,128)(2,1)S(1)}, bf16[72,768]{1,0:T(8,128)(2,1)S(1)}, u32[]{:S(2)}, u32[]{:S(2)}) collective-permute-start(bf16[72,768]{1,0:T(8,128)(2,1)S(1)} %get-tuple-element.35), channel_id=1, source_target_pairs={{0,2},{1,3},{2,0},{3,1},{4,6},{5,7},{6,4},{7,5},{8,10},{9,11},{10,... | collective-permute-start | bytes 331784 | tf_op jit(solution)/shard_map/ppermute | solution.py:373
  52.4 5.4 %collective-permute-start.15 = (bf16[72,768]{1,0:T(8,128)(2,1)S(1)}, bf16[72,768]{1,0:T(8,128)(2,1)S(1)}, u32[]{:S(2)}, u32[]{:S(2)}) collective-permute-start(bf16[72,768]{1,0:T(8,128)(2,1)S(1)} %get-tuple-element.36), channel_id=1, source_target_pairs={{0,3},{1,2},{2,1},{3,0},{4,7},{5,6},{6,5},{7,4},{8,11},{9,10},{10,... | collective-permute-start | bytes 331784 | tf_op jit(solution)/shard_map/ppermute | solution.py:373
  61.1 7.9 %collective-permute-start.16 = (bf16[72,512]{1,0:T(8,128)(2,1)}, bf16[72,512]{1,0:T(8,128)(2,1)S(1)}, u32[]{:S(2)}, u32[]{:S(2)}) collective-permute-start(bf16[72,512]{1,0:T(8,128)(2,1)} %get-tuple-element.38), channel_id=1, source_target_pairs={{0,4},{4,0},{8,12},{12,8},{16,20},{20,16},{24,28},{28,24},{1,5},{5... | collective-permute-start | bytes 221192 | tf_op jit(solution)/shard_map/ppermute | solution.py:376
  62.8 9.4 %collective-permute-start.17 = (bf16[72,512]{1,0:T(8,128)(2,1)}, bf16[72,512]{1,0:T(8,128)(2,1)S(1)}, u32[]{:S(2)}, u32[]{:S(2)}) collective-permute-start(bf16[72,512]{1,0:T(8,128)(2,1)} %get-tuple-element.39), channel_id=1, source_target_pairs={{0,8},{4,12},{8,0},{12,4},{16,24},{20,28},{24,16},{28,20},{1,9},{5... | collective-permute-start | bytes 221192 | tf_op jit(solution)/shard_map/ppermute | solution.py:376
  64.5 9.1 %collective-permute-start.18 = (bf16[72,512]{1,0:T(8,128)(2,1)}, bf16[72,512]{1,0:T(8,128)(2,1)S(1)}, u32[]{:S(2)}, u32[]{:S(2)}) collective-permute-start(bf16[72,512]{1,0:T(8,128)(2,1)} %copy-done.28), channel_id=1, source_target_pairs={{0,12},{4,8},{8,4},{12,0},{16,28},{20,24},{24,20},{28,16},{1,13},{... | collective-permute-start | bytes 221192 | tf_op jit(solution)/shard_map/ppermute | solution.py:376
  65.2 8.5 %collective-permute-start.19 = (bf16[72,512]{1,0:T(8,128)(2,1)}, bf16[72,512]{1,0:T(8,128)(2,1)}, u32[]{:S(2)}, u32[]{:S(2)}) collective-permute-start(bf16[72,512]{1,0:T(8,128)(2,1)} %copy-done.27), channel_id=1, source_target_pairs={{0,16},{4,20},{8,24},{12,28},{16,0},{20,4},{24,8},{28,12},{1,17},{... | collective-permute-start | bytes 221192 | tf_op jit(solution)/shard_map/ppermute | solution.py:376
  67.5 12.2 %collective-permute-start.20 = (bf16[72,512]{1,0:T(8,128)(2,1)}, bf16[72,512]{1,0:T(8,128)(2,1)}, u32[]{:S(2)}, u32[]{:S(2)}) collective-permute-start(bf16[72,512]{1,0:T(8,128)(2,1)} %copy-done.26), channel_id=1, source_target_pairs={{0,20},{4,16},{8,28},{12,24},{16,4},{20,0},{24,12},{28,8},{1,21},{... | collective-permute-start | bytes 221192 | tf_op jit(solution)/shard_map/ppermute | solution.py:376
  68.9 10.8 %collective-permute-start.21 = (bf16[72,512]{1,0:T(8,128)(2,1)}, bf16[72,512]{1,0:T(8,128)(2,1)}, u32[]{:S(2)}, u32[]{:S(2)}) collective-permute-start(bf16[72,512]{1,0:T(8,128)(2,1)} %copy-done.25), channel_id=1, source_target_pairs={{0,24},{4,28},{8,16},{12,20},{16,8},{20,12},{24,0},{28,4},{1,25},{... | collective-permute-start | bytes 221192 | tf_op jit(solution)/shard_map/ppermute | solution.py:376
  72.2 7.6 %collective-permute-start.22 = (bf16[72,512]{1,0:T(8,128)(2,1)}, bf16[72,512]{1,0:T(8,128)(2,1)}, u32[]{:S(2)}, u32[]{:S(2)}) collective-permute-start(bf16[72,512]{1,0:T(8,128)(2,1)} %copy-done.24), channel_id=1, source_target_pairs={{0,28},{4,24},{8,20},{12,16},{16,12},{20,8},{24,4},{28,0},{1,29},{... | collective-permute-start | bytes 221192 | tf_op jit(solution)/shard_map/ppermute | solution.py:376
  92.5 8.5 %collective-permute-start.23 = (bf16[72,512]{1,0:T(8,128)(2,1)}, bf16[72,512]{1,0:T(8,128)(2,1)S(1)}, u32[]{:S(2)}, u32[]{:S(2)}) collective-permute-start(bf16[72,512]{1,0:T(8,128)(2,1)} %get-tuple-element.47), channel_id=1, source_target_pairs={{0,4},{4,0},{8,12},{12,8},{16,20},{20,16},{24,28},{28,24},{1,5},{5... | collective-permute-start | bytes 221192 | tf_op jit(solution)/shard_map/ppermute | solution.py:376
  93.3 10.1 %collective-permute-start.24 = (bf16[72,512]{1,0:T(8,128)(2,1)}, bf16[72,512]{1,0:T(8,128)(2,1)S(1)}, u32[]{:S(2)}, u32[]{:S(2)}) collective-permute-start(bf16[72,512]{1,0:T(8,128)(2,1)} %get-tuple-element.48), channel_id=1, source_target_pairs={{0,8},{4,12},{8,0},{12,4},{16,24},{20,28},{24,16},{28,20},{1,9},{5... | collective-permute-start | bytes 221192 | tf_op jit(solution)/shard_map/ppermute | solution.py:376
  96.8 14.6 %collective-permute-start.25 = (bf16[72,512]{1,0:T(8,128)(2,1)}, bf16[72,512]{1,0:T(8,128)(2,1)S(1)}, u32[]{:S(2)}, u32[]{:S(2)}) collective-permute-start(bf16[72,512]{1,0:T(8,128)(2,1)} %copy-done.23), channel_id=1, source_target_pairs={{0,12},{4,8},{8,4},{12,0},{16,28},{20,24},{24,20},{28,16},{1,13},{... | collective-permute-start | bytes 221192 | tf_op jit(solution)/shard_map/ppermute | solution.py:376
  97.4 14.0 %collective-permute-start.26 = (bf16[72,512]{1,0:T(8,128)(2,1)}, bf16[72,512]{1,0:T(8,128)(2,1)S(1)}, u32[]{:S(2)}, u32[]{:S(2)}) collective-permute-start(bf16[72,512]{1,0:T(8,128)(2,1)} %copy-done.22), channel_id=1, source_target_pairs={{0,16},{4,20},{8,24},{12,28},{16,0},{20,4},{24,8},{28,12},{1,17},{... | collective-permute-start | bytes 221192 | tf_op jit(solution)/shard_map/ppermute | solution.py:376
  100.7 11.1 %collective-permute-start.27 = (bf16[72,512]{1,0:T(8,128)(2,1)}, bf16[72,512]{1,0:T(8,128)(2,1)S(1)}, u32[]{:S(2)}, u32[]{:S(2)}) collective-permute-start(bf16[72,512]{1,0:T(8,128)(2,1)} %copy-done.21), channel_id=1, source_target_pairs={{0,20},{4,16},{8,28},{12,24},{16,4},{20,0},{24,12},{28,8},{1,21},{... | collective-permute-start | bytes 221192 | tf_op jit(solution)/shard_map/ppermute | solution.py:376
  101.0 10.8 %collective-permute-start.28 = (bf16[72,512]{1,0:T(8,128)(2,1)}, bf16[72,512]{1,0:T(8,128)(2,1)S(1)}, u32[]{:S(2)}, u32[]{:S(2)}) collective-permute-start(bf16[72,512]{1,0:T(8,128)(2,1)} %copy-done.20), channel_id=1, source_target_pairs={{0,24},{4,28},{8,16},{12,20},{16,8},{20,12},{24,0},{28,4},{1,25},{... | collective-permute-start | bytes 221192 | tf_op jit(solution)/shard_map/ppermute | solution.py:376
  103.4 8.4 %collective-permute-start.29 = (bf16[72,512]{1,0:T(8,128)(2,1)}, bf16[72,512]{1,0:T(8,128)(2,1)S(1)}, u32[]{:S(2)}, u32[]{:S(2)}) collective-permute-start(bf16[72,512]{1,0:T(8,128)(2,1)} %copy-done.19), channel_id=1, source_target_pairs={{0,28},{4,24},{8,20},{12,16},{16,12},{20,8},{24,4},{28,0},{1,29},{... | collective-permute-start | bytes 221192 | tf_op jit(solution)/shard_map/ppermute | solution.py:376
  107.2 21.8 %all-to-all-start.3 = ((bf16[8,72,512]{2,1,0:T(8,128)(2,1)}), bf16[8,72,512]{2,1,0:T(8,128)(2,1)}, u32[]{:S(2)}, u32[]{:S(2)}) async-start(bf16[8,72,512]{2,1,0:T(8,128)(2,1)} %bitcast.56), calls=%async_computation.3 | async-start | bytes 1179648 | tf_op jit(solution)/shard_map/all_to_all | solution.py:379
  112.7 1.9 collective-permute-start.30
  112.8 6.0 %collective-permute-start.31 = (bf16[72,768]{1,0:T(8,128)(2,1)S(1)}, bf16[72,768]{1,0:T(8,128)(2,1)S(1)}, u32[]{:S(2)}, u32[]{:S(2)}) collective-permute-start(bf16[72,768]{1,0:T(8,128)(2,1)S(1)} %get-tuple-element.56), channel_id=1, source_target_pairs={{0,2},{1,3},{2,0},{3,1},{4,6},{5,7},{6,4},{7,5},{8,10},{9,11},{10,... | collective-permute-start | bytes 331784 | tf_op jit(solution)/shard_map/ppermute | solution.py:373
  114.3 5.7 %collective-permute-start.32 = (bf16[72,768]{1,0:T(8,128)(2,1)S(1)}, bf16[72,768]{1,0:T(8,128)(2,1)S(1)}, u32[]{:S(2)}, u32[]{:S(2)}) collective-permute-start(bf16[72,768]{1,0:T(8,128)(2,1)S(1)} %get-tuple-element.57), channel_id=1, source_target_pairs={{0,3},{1,2},{2,1},{3,0},{4,7},{5,6},{6,5},{7,4},{8,11},{9,10},{10,... | collective-permute-start | bytes 331784 | tf_op jit(solution)/shard_map/ppermute | solution.py:373
  128.1 14.7 %collective-permute-start.35 = (bf16[2,8,4096]{2,1,0:T(8,128)(2,1)S(1)}, bf16[2,8,4096]{2,1,0:T(8,128)(2,1)S(1)}, u32[]{:S(2)}, u32[]{:S(2)}) collective-permute-start(bf16[2,8,4096]{2,1,0:T(8,128)(2,1)S(1)} %get-tuple-element.62), channel_id=1, source_target_pairs={{0,1},{1,0},{2,3},{3,2},{4,5},{5,4},{6,7},{7,6},{8,9},{9,8},{10,11... | collective-permute-start | bytes 393224 | tf_op jit(solution)/shard_map/ppermute | solution.py:373
  129.0 36.8 %collective-permute-start.37 = (bf16[8,72,512]{2,1,0:T(8,128)(2,1)}, bf16[8,72,512]{2,1,0:T(8,128)(2,1)}, u32[]{:S(2)}, u32[]{:S(2)}) collective-permute-start(bf16[8,72,512]{2,1,0:T(8,128)(2,1)} %all-to-all-done.3), channel_id=1, source_target_pairs={{0,1},{1,0},{2,3},{3,2},{4,5},{5,4},{6,7},{7,6},{8,9},{9,8},{10,11... | collective-permute-start | bytes 1769480 | tf_op jit(solution)/shard_map/ppermute | solution.py:373
  131.5 57.8 %all-to-all-start.1 = ((bf16[8,72,256]{2,1,0:T(8,128)(2,1)}), bf16[8,72,256]{2,1,0:T(8,128)(2,1)S(1)}, u32[]{:S(2)}, u32[]{:S(2)}) async-start(bf16[8,72,256]{2,1,0:T(8,128)(2,1)} %bitcast.10), calls=%async_computation.1 | async-start | bytes 589824 | tf_op jit(solution)/shard_map/all_to_all | solution.py:379
  142.8 7.2 %collective-permute-start.33 = (bf16[2,64,4096]{2,1,0:T(8,128)(2,1)}, bf16[2,64,4096]{2,1,0:T(8,128)(2,1)S(1)}, u32[]{:S(2)}, u32[]{:S(2)}) collective-permute-start(bf16[2,64,4096]{2,1,0:T(8,128)(2,1)} %copy-done.18), channel_id=1, source_target_pairs={{0,1},{1,0},{2,3},{3,2},{4,5},{5,4},{6,7},{7,6},{8,9},{9,8},{10,11... | collective-permute-start | bytes 3145736 | tf_op jit(solution)/shard_map/ppermute | solution.py:373
  142.9 5.6 %collective-permute-start.36 = (bf16[8,4096]{1,0:T(8,128)(2,1)S(1)}, bf16[8,4096]{1,0:T(8,128)(2,1)S(1)}, u32[]{:S(2)}, u32[]{:S(2)}) collective-permute-start(bf16[8,4096]{1,0:T(8,128)(2,1)S(1)} %slice_bitcast_fusion.2), channel_id=1, source_target_pairs={{0,2},{1,3},{2,0},{3,1},{4,6},{5,7},{6,4},{7,5},{8,10},{9,11},{10,... | collective-permute-start | bytes 196616 | tf_op jit(solution)/shard_map/ppermute | solution.py:373
  145.0 12.8 %collective-permute-start.43 = (bf16[288,384]{1,0:T(8,128)(2,1)S(1)}, bf16[288,384]{1,0:T(8,128)(2,1)S(1)}, u32[]{:S(2)}, u32[]{:S(2)}) collective-permute-start(bf16[288,384]{1,0:T(8,128)(2,1)S(1)} %pad_maximum_fusion.3.refs_1_), channel_id=1, source_target_pairs={{0,8},{4,12},{8,16},{12,20},{16,24},{20,28},{24,0},{28,4},{1,9},{5... | collective-permute-start | bytes 663560 | tf_op jit(solution)/shard_map/ppermute | solution.py:376
  147.0 14.7 %collective-permute-start.40 = (bf16[288,384]{1,0:T(8,128)(2,1)S(1)}, bf16[288,384]{1,0:T(8,128)(2,1)S(1)}, u32[]{:S(2)}, u32[]{:S(2)}) collective-permute-start(bf16[288,384]{1,0:T(8,128)(2,1)S(1)} %pad_maximum_fusion.2.refs_0_), channel_id=1, source_target_pairs={{0,8},{4,12},{8,16},{12,20},{16,24},{20,28},{24,0},{28,4},{1,9},{5... | collective-permute-start | bytes 663560 | tf_op jit(solution)/shard_map/ppermute | solution.py:376
  148.5 13.2 %collective-permute-start.49 = (bf16[288,384]{1,0:T(8,128)(2,1)S(1)}, bf16[288,384]{1,0:T(8,128)(2,1)S(1)}, u32[]{:S(2)}, u32[]{:S(2)}) collective-permute-start(bf16[288,384]{1,0:T(8,128)(2,1)S(1)} %pad_maximum_fusion.3.refs_1_), channel_id=1, source_target_pairs={{0,4},{4,0},{8,12},{12,8},{16,20},{20,16},{24,28},{28,24},{1,5},{5... | collective-permute-start | bytes 663560 | tf_op jit(solution)/shard_map/ppermute | solution.py:376
  150.0 13.3 %collective-permute-start.48 = (bf16[288,384]{1,0:T(8,128)(2,1)S(1)}, bf16[288,384]{1,0:T(8,128)(2,1)S(1)}, u32[]{:S(2)}, u32[]{:S(2)}) collective-permute-start(bf16[288,384]{1,0:T(8,128)(2,1)S(1)} %pad_maximum_fusion.2.refs_0_), channel_id=1, source_target_pairs={{0,4},{4,0},{8,12},{12,8},{16,20},{20,16},{24,28},{28,24},{1,5},{5... | collective-permute-start | bytes 663560 | tf_op jit(solution)/shard_map/ppermute | solution.py:376
  152.1 36.1 %copy-start.29 = (bf16[2,64,4096]{2,1,0:T(8,128)(2,1)}, bf16[2,64,4096]{2,1,0:T(8,128)(2,1)S(1)}, u32[]{:S(2)}) copy-start(bf16[2,64,4096]{2,1,0:T(8,128)(2,1)S(1)} %add_convert_fusion) | copy-start | bytes 3145732
  157.8 30.4 %copy-start.4 = (bf16[288,384]{1,0:T(8,128)(2,1)}, bf16[288,384]{1,0:T(8,128)(2,1)S(1)}, u32[]{:S(2)}) copy-start(bf16[288,384]{1,0:T(8,128)(2,1)S(1)} %collective-permute-done.43.refs_5_) | copy-start | bytes 663556
  157.8 13.8 %collective-permute-start.38 = (bf16[8,72,512]{2,1,0:T(8,128)(2,1)}, bf16[8,72,512]{2,1,0:T(8,128)(2,1)S(1)}, u32[]{:S(2)}, u32[]{:S(2)}) collective-permute-start(bf16[8,72,512]{2,1,0:T(8,128)(2,1)} %all-to-all-done.3), channel_id=1, source_target_pairs={{0,2},{1,3},{2,0},{3,1},{4,6},{5,7},{6,4},{7,5},{8,10},{9,11},{10,... | collective-permute-start | bytes 1769480 | tf_op jit(solution)/shard_map/ppermute | solution.py:373
  161.7 26.6 %copy-start.6 = (bf16[288,384]{1,0:T(8,128)(2,1)}, bf16[288,384]{1,0:T(8,128)(2,1)S(1)}, u32[]{:S(2)}) copy-start(bf16[288,384]{1,0:T(8,128)(2,1)S(1)} %collective-permute-done.40.refs_4_) | copy-start | bytes 663556
  161.7 10.2 %collective-permute-start.44 = (bf16[288,384]{1,0:T(8,128)(2,1)S(1)}, bf16[288,384]{1,0:T(8,128)(2,1)}, u32[]{:S(2)}, u32[]{:S(2)}) collective-permute-start(bf16[288,384]{1,0:T(8,128)(2,1)S(1)} %collective-permute-done.43.refs_5_), channel_id=1, source_target_pairs={{0,8},{4,12},{8,16},{12,20},{16,24},{20,28},{24,0},{28,4},{1,9},{5... | collective-permute-start | bytes 663560 | tf_op jit(solution)/shard_map/ppermute | solution.py:376
  161.7 26.6 %copy-start.8 = (bf16[288,384]{1,0:T(8,128)(2,1)}, bf16[288,384]{1,0:T(8,128)(2,1)S(1)}, u32[]{:S(2)}) copy-start(bf16[288,384]{1,0:T(8,128)(2,1)S(1)} %collective-permute-done.49.refs_3_) | copy-start | bytes 663556
  161.7 13.2 %collective-permute-start.51 = (bf16[288,384]{1,0:T(8,128)(2,1)S(1)}, bf16[288,384]{1,0:T(8,128)(2,1)S(1)}, u32[]{:S(2)}, u32[]{:S(2)}) collective-permute-start(bf16[288,384]{1,0:T(8,128)(2,1)S(1)} %collective-permute-done.43.refs_5_), channel_id=1, source_target_pairs={{0,4},{4,0},{8,12},{12,8},{16,20},{20,16},{24,28},{28,24},{1,5},{5... | collective-permute-start | bytes 663560 | tf_op jit(solution)/shard_map/ppermute | solution.py:376
  163.2 25.0 %copy-start.10 = (bf16[288,384]{1,0:T(8,128)(2,1)}, bf16[288,384]{1,0:T(8,128)(2,1)S(1)}, u32[]{:S(2)}) copy-start(bf16[288,384]{1,0:T(8,128)(2,1)S(1)} %collective-permute-done.48.refs_2_) | copy-start | bytes 663556
  163.2 11.6 %collective-permute-start.41 = (bf16[288,384]{1,0:T(8,128)(2,1)S(1)}, bf16[288,384]{1,0:T(8,128)(2,1)}, u32[]{:S(2)}, u32[]{:S(2)}) collective-permute-start(bf16[288,384]{1,0:T(8,128)(2,1)S(1)} %collective-permute-done.40.refs_4_), channel_id=1, source_target_pairs={{0,8},{4,12},{8,16},{12,20},{16,24},{20,28},{24,0},{28,4},{1,9},{5... | collective-permute-start | bytes 663560 | tf_op jit(solution)/shard_map/ppermute | solution.py:376
  165.8 14.1 %collective-permute-start.50 = (bf16[288,384]{1,0:T(8,128)(2,1)S(1)}, bf16[288,384]{1,0:T(8,128)(2,1)S(1)}, u32[]{:S(2)}, u32[]{:S(2)}) collective-permute-start(bf16[288,384]{1,0:T(8,128)(2,1)S(1)} %collective-permute-done.40.refs_4_), channel_id=1, source_target_pairs={{0,4},{4,0},{8,12},{12,8},{16,20},{20,16},{24,28},{28,24},{1,5},{5... | collective-permute-start | bytes 663560 | tf_op jit(solution)/shard_map/ppermute | solution.py:376
  171.6 16.1 %collective-permute-start.39 = (bf16[8,72,512]{2,1,0:T(8,128)(2,1)S(1)}, bf16[8,72,512]{2,1,0:T(8,128)(2,1)S(1)}, u32[]{:S(2)}, u32[]{:S(2)}) collective-permute-start(bf16[8,72,512]{2,1,0:T(8,128)(2,1)S(1)} %collective-permute-done.38), channel_id=1, source_target_pairs={{0,1},{1,0},{2,3},{3,2},{4,5},{5,4},{6,7},{7,6},{8,9},{9,8},{10,11... | collective-permute-start | bytes 1769480 | tf_op jit(solution)/shard_map/ppermute | solution.py:373
  171.9 10.3 %collective-permute-start.45 = (bf16[288,384]{1,0:T(8,128)(2,1)}, bf16[288,384]{1,0:T(8,128)(2,1)S(1)}, u32[]{:S(2)}, u32[]{:S(2)}) collective-permute-start(bf16[288,384]{1,0:T(8,128)(2,1)} %collective-permute-done.44.refs_9_), channel_id=1, source_target_pairs={{0,8},{4,12},{8,16},{12,20},{16,24},{20,28},{24,0},{28,4},{1,9},{5... | collective-permute-start | bytes 663560 | tf_op jit(solution)/shard_map/ppermute | solution.py:376
  174.9 11.3 %collective-permute-start.42 = (bf16[288,384]{1,0:T(8,128)(2,1)}, bf16[288,384]{1,0:T(8,128)(2,1)S(1)}, u32[]{:S(2)}, u32[]{:S(2)}) collective-permute-start(bf16[288,384]{1,0:T(8,128)(2,1)} %collective-permute-done.41.refs_8_), channel_id=1, source_target_pairs={{0,8},{4,12},{8,16},{12,20},{16,24},{20,28},{24,0},{28,4},{1,9},{5... | collective-permute-start | bytes 663560 | tf_op jit(solution)/shard_map/ppermute | solution.py:376
  175.5 35.4 %collective-permute-start.34 = (bf16[64,4096]{1,0:T(8,128)(2,1)}, bf16[64,4096]{1,0:T(8,128)(2,1)}, u32[]{:S(2)}, u32[]{:S(2)}) collective-permute-start(bf16[64,4096]{1,0:T(8,128)(2,1)} %slice_bitcast_fusion), channel_id=1, source_target_pairs={{0,2},{1,3},{2,0},{3,1},{4,6},{5,7},{6,4},{7,5},{8,10},{9,11},{10,... | collective-permute-start | bytes 1572872 | tf_op jit(solution)/shard_map/ppermute | solution.py:373
  180.6 15.6 %collective-permute-start.53 = (bf16[288,384]{1,0:T(8,128)(2,1)}, bf16[288,384]{1,0:T(8,128)(2,1)}, u32[]{:S(2)}, u32[]{:S(2)}) collective-permute-start(bf16[288,384]{1,0:T(8,128)(2,1)} %collective-permute-done.44.refs_9_), channel_id=1, source_target_pairs={{0,4},{4,0},{8,12},{12,8},{16,20},{20,16},{24,28},{28,24},{1,5},{5... | collective-permute-start | bytes 663560 | tf_op jit(solution)/shard_map/ppermute | solution.py:376
  182.2 14.0 %collective-permute-start.52 = (bf16[288,384]{1,0:T(8,128)(2,1)}, bf16[288,384]{1,0:T(8,128)(2,1)}, u32[]{:S(2)}, u32[]{:S(2)}) collective-permute-start(bf16[288,384]{1,0:T(8,128)(2,1)} %collective-permute-done.41.refs_8_), channel_id=1, source_target_pairs={{0,4},{4,0},{8,12},{12,8},{16,20},{20,16},{24,28},{28,24},{1,5},{5... | collective-permute-start | bytes 663560 | tf_op jit(solution)/shard_map/ppermute | solution.py:376
  186.2 20.6 %collective-permute-start.47 = (bf16[288,384]{1,0:T(8,128)(2,1)S(1)}, bf16[288,384]{1,0:T(8,128)(2,1)S(1)}, u32[]{:S(2)}, u32[]{:S(2)}) collective-permute-start(bf16[288,384]{1,0:T(8,128)(2,1)S(1)} %collective-permute-done.45.refs_1_), channel_id=1, source_target_pairs={{0,4},{4,0},{8,12},{12,8},{16,20},{20,16},{24,28},{28,24},{1,5},{5... | collective-permute-start | bytes 663560 | tf_op jit(solution)/shard_map/ppermute | solution.py:376
  187.7 19.2 %collective-permute-start.46 = (bf16[288,384]{1,0:T(8,128)(2,1)S(1)}, bf16[288,384]{1,0:T(8,128)(2,1)}, u32[]{:S(2)}, u32[]{:S(2)}) collective-permute-start(bf16[288,384]{1,0:T(8,128)(2,1)S(1)} %collective-permute-done.42.refs_0_), channel_id=1, source_target_pairs={{0,4},{4,0},{8,12},{12,8},{16,20},{20,16},{24,28},{28,24},{1,5},{5... | collective-permute-start | bytes 663560 | tf_op jit(solution)/shard_map/ppermute | solution.py:376
  189.3 22.7 %all-to-all-start.2 = ((bf16[8,8,4096]{2,1,0:T(8,128)(2,1)}), bf16[8,8,4096]{2,1,0:T(8,128)(2,1)}, u32[]{:S(2)}, u32[]{:S(2)}) async-start(bf16[8,8,4096]{2,1,0:T(8,128)(2,1)} %broadcast_select_fusion), calls=%async_computation.2 | async-start | bytes 1048576 | tf_op jit(solution)/shard_map/all_to_all | solution.py:379
  (36 other events, 140.8 us)
